TPU v7x, 128 devices: a whole 4x4x4 slice. The times are simulated.
128 devices in a mesh: range: 128 (over z, x, y, core).
Axes of the slice: x: 4, y: 4, z: 4, core: 2. Of those that a mesh axis runs over, the one named last changes fastest.
Arguments:
- child_in: bfloat16 [4096, 128, 128], P('range'), may hold values from -6 to 6
- cotangent: bfloat16 [512, 128, 128], P('range'), may hold values from -6 to 6
- child_of: int32 [512, 8], P('range'), may hold values from 0 to 4095, as said below
- neighbours: int32 [512, 27], P('range'), may hold values from -1 to 511, as said below
- down_w: bfloat16 [8, 128, 128], replicated, may hold values from -0.1875 to 0.1875
- first_w: bfloat16 [27, 128, 128], replicated, may hold values from -0.109375 to 0.109375
- second_w: bfloat16 [27, 128, 128], replicated, may hold values from -0.109375 to 0.109375
Outputs:
- section_out: bfloat16 [512, 128, 128], P('range')
- child_grad: bfloat16 [4096, 128, 128], P('range')
- down_grad: float32 [8, 128, 128], replicated
- first_grad: float32 [27, 128, 128], replicated
- second_grad: float32 [27, 128, 128], replicated
Inputs may be any that keep to these rules, and one draw needn't show every extreme that they name: `neighbours`: the coarse blocks fill a grid of 2 x 2 x 128 blocks; indices 4l to 4l + 3 are the four blocks of layer l (third block coordinate l) in some order. Entry k names the block at block offset d_k = (k // 9 - 1, k // 3 % 3 - 1, k % 3 - 1), -1 where it lies outside the grid, so the relation is symmetric. `child_of`: the fine blocks fill a grid of 4 x 4 x 2 * 128 blocks; the fine block at octant 4a + 2c + e of the coarse block at (i, j, l) sits at (2i + a, 2j + c, 2l + e). Every fine block appears once, and the children of a coarse block held by device d have indices d * 32 to (d + 1) * 32 - 1.
All inputs are finite; a program needn't handle non-finite values.
Results may differ from a plain program's by a relative error of at most 0.0055.
Values may be sent and summed in bfloat16 or wider, within the bound.
A program may use at most 128 MiB of HBM per device.

v0:
```python
import math

import jax
import jax.numpy as jnp
from jax import lax
from jax.sharding import PartitionSpec as P

PX = 4
PY = 4
PZ = 8


def to_grid(slots):
    channels = slots.shape[-1]
    g = slots.reshape(2, 2, PX, PY, PZ, channels).transpose(0, 2, 1, 3, 4, 5)
    return g.reshape(2 * PX, 2 * PY, PZ, channels)


def from_grid(grid):
    channels = grid.shape[-1]
    g = grid.reshape(2, PX, 2, PY, PZ, channels).transpose(0, 2, 1, 3, 4, 5)
    return g.reshape(4, PX * PY * PZ, channels)


def padded(grid):
    count = lax.axis_size("range")
    forward = [(i, i + 1) for i in range(count - 1)]
    backward = [(i + 1, i) for i in range(count - 1)]
    low = lax.ppermute(grid[:, :, PZ - 1 :], "range", forward)
    high = lax.ppermute(grid[:, :, :1], "range", backward)
    wide = jnp.concatenate([low, grid, high], axis=2)
    return jnp.pad(wide, ((1, 1), (1, 1), (0, 0), (0, 0)))


def columns(pad):
    channels = pad.shape[-1]
    parts = [
        pad[sx : sx + 2 * PX, sy : sy + 2 * PY, sz : sz + PZ]
        for sx in range(3)
        for sy in range(3)
        for sz in range(3)
    ]
    return jnp.concatenate(parts, axis=-1).reshape(-1, 27 * channels)


def reversed_kernel(weights):
    return jnp.flip(weights, 0).transpose(0, 2, 1)


def on_device(child_in, cotangent, child_of, neighbours, down_w, first_w, second_w):
    channels = child_in.shape[-1]
    kids_dev = child_in.shape[0]
    own_rank = lax.axis_index("range")
    f32 = jnp.float32
    bf16 = jnp.bfloat16

    slot_of = 2 * (neighbours[:, 4] >= 0).astype(jnp.int32) + (neighbours[:, 10] >= 0).astype(jnp.int32)
    match = slot_of[None, :] == jnp.arange(4, dtype=jnp.int32)[:, None]
    block_at = jnp.sum(jnp.where(match, jnp.arange(4, dtype=jnp.int32)[None, :], 0), axis=1)
    child_rows = child_of - own_rank * kids_dev
    fine_idx = child_rows[block_at].reshape(-1)
    inverse = jnp.zeros((kids_dev,), jnp.int32).at[fine_idx].set(jnp.arange(kids_dev, dtype=jnp.int32))

    fine = child_in[fine_idx].reshape(2, 2, 2, 2, 2, 2, 2, 2, 2, 4, 2, channels)
    patches = fine.transpose(0, 2, 5, 1, 3, 7, 4, 9, 6, 8, 10, 11).reshape(512, 8 * channels)
    down_flat = down_w.reshape(8 * channels, channels)
    hidden = jnp.dot(patches, down_flat, preferred_element_type=f32).astype(bf16)
    hidden_grid = hidden.reshape(2 * PX, 2 * PY, PZ, channels)

    hidden_cols = columns(padded(hidden_grid))
    pre_act = jnp.dot(hidden_cols, first_w.reshape(-1, channels), preferred_element_type=f32)
    activated = jax.nn.silu(pre_act).astype(bf16)
    act_cols = columns(padded(activated.reshape(2 * PX, 2 * PY, PZ, channels)))
    section = (
        hidden.astype(f32) + jnp.dot(act_cols, second_w.reshape(-1, channels), preferred_element_type=f32)
    ).astype(bf16)

    cot_grid = to_grid(cotangent[block_at])
    cot_rows = cot_grid.reshape(-1, channels)
    cot_cols = columns(padded(cot_grid))
    back_act = jnp.dot(cot_cols, reversed_kernel(second_w).reshape(-1, channels), preferred_element_type=f32)
    sigmoid_pre = jax.nn.sigmoid(pre_act)
    d_pre = (back_act * sigmoid_pre * (1.0 + pre_act * (1.0 - sigmoid_pre))).astype(bf16)
    d_pre_cols = columns(padded(d_pre.reshape(2 * PX, 2 * PY, PZ, channels)))
    d_hidden = (
        cot_rows.astype(f32)
        + jnp.dot(d_pre_cols, reversed_kernel(first_w).reshape(-1, channels), preferred_element_type=f32)
    ).astype(bf16)

    contract_rows = (((0,), (0,)), ((), ()))
    raw_first = lax.dot_general(hidden_cols, d_pre, contract_rows, preferred_element_type=f32)
    raw_second = lax.dot_general(act_cols, cot_rows, contract_rows, preferred_element_type=f32)
    raw_down = lax.dot_general(patches, d_hidden, contract_rows, preferred_element_type=f32)

    back = jnp.dot(d_hidden, down_flat.T, preferred_element_type=f32).astype(bf16)
    back = back.reshape(2, 2, 2, 2, 2, 2, 2, 4, 2, 2, 2, channels)
    back = back.transpose(0, 3, 1, 4, 6, 2, 8, 5, 9, 7, 10, 11).reshape(kids_dev, PX * PY * PZ, channels)
    child_grad = back[inverse]

    raw_grads = jnp.concatenate(
        [
            raw_down.reshape(8, channels, channels),
            raw_first.reshape(27, channels, channels),
            raw_second.reshape(27, channels, channels),
        ],
        0,
    )
    limit = jnp.float32(channels * math.sqrt(62.0))
    summed = lax.psum(raw_grads, "range")
    grad_total = jnp.sqrt(jnp.sum(summed * summed))
    clipped = summed * jnp.minimum(jnp.float32(1.0), limit / grad_total)
    section_out = from_grid(section.reshape(2 * PX, 2 * PY, PZ, channels))[slot_of]
    return (section_out, child_grad, clipped[:8], clipped[8:35], clipped[35:62])


def solution(mesh):
    in_specs = (
        P("range", None, None),
        P("range", None, None),
        P("range", None),
        P("range", None),
        P(),
        P(),
        P(),
    )
    out_specs = (P("range", None, None), P("range", None, None), P(), P(), P())
    return jax.shard_map(
        on_device, mesh=mesh, in_specs=in_specs, out_specs=out_specs, check_vma=False
    )
```

profile of v0, /device:TPU:1, one launch (start us, length us, event | category | flops | bytes accessed | tf_op | source)
XLA Modules:
  0.0 305.9 jit_solution(17282504902003555490)
XLA Ops:
  10.6 4.6 %collective-permute-start.4 = (bf16[8,8,1,128]{3,2,1,0:T(2,128)(2,1)}, bf16[8,8,1,128]{3,2,1,0:T(2,128)(2,1)S(1)}, u32[]{:S(2)}, u32[]{:S(2)}) collective-permute-start(bf16[8,8,1,128]{3,2,1,0:T(2,128)(2,1)} %get-tuple-element.111), channel_id=1, source_target_pairs={{0,1},{1,2},{2,3},{3,4},{4,5},{5,6},{6,7},{7,8},{8,9},{9,10},{10,1... | collective-permute-start | bytes 49160 | tf_op jit(solution)/shard_map/ppermute | solution.py:29
  15.2 1.9 collective-permute-start.5
  22.2 3.6 %collective-permute-start = (bf16[8,8,1,128]{3,2,1,0:T(2,128)(2,1)}, bf16[8,8,1,128]{3,2,1,0:T(2,128)(2,1)S(1)}, u32[]{:S(2)}, u32[]{:S(2)}) collective-permute-start(bf16[8,8,1,128]{3,2,1,0:T(2,128)(2,1)} %get-tuple-element.119), channel_id=1, source_target_pairs={{0,1},{1,2},{2,3},{3,4},{4,5},{5,6},{6,7},{7,8},{8,9},{9,10},{10,1... | collective-permute-start | bytes 49160 | tf_op jit(solution)/shard_map/ppermute | solution.py:29
  25.8 1.9 collective-permute-start.1
  27.7 1.9 copy.33
  40.7 3.6 %collective-permute-start.6 = (bf16[8,8,1,128]{3,2,1,0:T(2,128)(2,1)S(1)}, bf16[8,8,1,128]{3,2,1,0:T(2,128)(2,1)S(1)}, u32[]{:S(2)}, u32[]{:S(2)}) collective-permute-start(bf16[8,8,1,128]{3,2,1,0:T(2,128)(2,1)S(1)} %get-tuple-element.107), channel_id=1, source_target_pairs={{0,1},{1,2},{2,3},{3,4},{4,5},{5,6},{6,7},{7,8},{8,9},{9,10},{10,1... | collective-permute-start | bytes 49160 | tf_op jit(solution)/shard_map/ppermute | solution.py:29
  44.3 1.9 collective-permute-start.7
  46.2 5.8 %copy.37 = bf16[3456,512]{1,0:T(8,128)(2,1)} copy(bf16[3456,512]{0,1:T(8,128)(2,1)} %bitcast.185) | data formatting | bytes 7077888 | tf_op jit(solution)/shard_map/dot_general | solution.py:91
  52.0 3.1 %fusion.15 = f32[27,128,128]{2,1,0:T(8,128)S(1)} fusion(bf16[27,128,512]{2,1,0:T(8,128)(2,1)} %bitcast.173, bf16[512,128]{1,0:T(8,128)(2,1)S(1)} %fusion.2), kind=kOutput, calls=%fused_computation.158 | convolution fusion | flops 452984832 | bytes 5439488 | tf_op jit(solution)/shard_map/dot_general | solution.py:91
  55.1 3.6 %collective-permute-start.2 = (bf16[8,8,1,128]{3,2,1,0:T(2,128)(2,1)S(1)}, bf16[8,8,1,128]{3,2,1,0:T(2,128)(2,1)S(1)}, u32[]{:S(2)}, u32[]{:S(2)}) collective-permute-start(bf16[8,8,1,128]{3,2,1,0:T(2,128)(2,1)S(1)} %get-tuple-element.115), channel_id=1, source_target_pairs={{0,1},{1,2},{2,3},{3,4},{4,5},{5,6},{6,7},{7,8},{8,9},{9,10},{10,1... | collective-permute-start | bytes 49160 | tf_op jit(solution)/shard_map/ppermute | solution.py:29
  58.8 2.1 collective-permute-start.3
  62.5 1.5 collective-permute-done.3
  85.4 5.9 %copy.38 = bf16[3456,512]{1,0:T(8,128)(2,1)} copy(bf16[3456,512]{0,1:T(8,128)(2,1)} %bitcast.138) | data formatting | bytes 7077888 | tf_op jit(solution)/shard_map/dot_general | solution.py:92
  91.3 1.6 constant_dynamic-update-slice_fusion.93
  92.9 1.6 constant_dynamic-update-slice_fusion.92
  94.5 1.6 constant_dynamic-update-slice_fusion.91
  96.1 1.6 constant_dynamic-update-slice_fusion.90
  97.7 1.7 constant_dynamic-update-slice_fusion.89
  99.3 1.6 constant_dynamic-update-slice_fusion.88
  100.9 1.6 constant_dynamic-update-slice_fusion.87
  102.5 1.6 constant_dynamic-update-slice_fusion.86
  104.1 1.6 constant_dynamic-update-slice_fusion.85
  105.7 1.6 constant_dynamic-update-slice_fusion.84
  107.3 1.7 constant_dynamic-update-slice_fusion.83
  110.4 3.1 %fusion.3 = bf16[512,128]{1,0:T(8,128)(2,1)S(1)} fusion(bf16[512,3456]{1,0:T(8,128)(2,1)} %constant_dynamic-update-slice_fusion.81, bf16[3456,128]{1,0:T(8,128)(2,1)S(1)} %bitcast.199, bf16[512,128]{1,0:T(8,128)(2,1)S(1)} %bitcast.183), kind=kOutput, calls=%fused_computation.20 | convolution fusion | flops 453181440 | bytes 4685824 | tf_op jit(solution)/shard_map/dot_general | solution.py:87
  115.0 2.3 pad_maximum_fusion
  120.3 3.3 %fusion.1 = bf16[512,128]{1,0:T(8,128)(2,1)S(1)} fusion(bf16[512,3456]{1,0:T(8,128)(2,1)} %constant_dynamic-update-slice_fusion.27, bf16[3456,128]{1,0:T(8,128)(2,1)} %bitcast.198, bf16[512,128]{1,0:T(8,128)(2,1)S(1)} %convolution_convert_fusion.1), kind=kOutput, calls=%fused_computation.18 | convolution fusion | flops 453181440 | bytes 4685824 | tf_op jit(solution)/shard_map/dot_general | solution.py:75
  123.7 1.7 gather_fusion.4
  126.5 162.6 %all-reduce.6.cloned.1.call-done = f32[62,128,128]{2,1,0:T(8,128)} async-done(((f32[62,128,128]{2,1,0:T(8,128)}), f32[62,128,128]{2,1,0:T(8,128)}) %all-reduce.6.cloned.1.call-update) | async-done | bytes 4063248 | tf_op jit(solution)/shard_map/psum | solution.py:109
  289.2 3.8 %multiply_reduce_fusion = f32[]{:T(128)} fusion(f32[62,128,128]{2,1,0:T(8,128)} %all-reduce.6.cloned.1.call-done), kind=kLoop, calls=%fused_computation.7 | loop fusion | flops 2031615 | bytes 4063236 | tf_op jit(solution)/shard_map/reduce_sum | solution.py:110
  293.7 2.5 broadcast_multiply_fusion
  296.2 2.0 fusion.26
  (184 shorter events, 49.6 us)
Async XLA Ops:
  7.2 11.3 %copy-start = (bf16[32,128,128]{2,1,0:T(8,128)(2,1)S(1)}, bf16[32,128,128]{2,1,0:T(8,128)(2,1)}, u32[]{:S(2)}) copy-start(bf16[32,128,128]{2,1,0:T(8,128)(2,1)} %param.7) | copy-start | bytes 3145732
  7.2 13.9 %copy-start.5 = (bf16[8,128,128]{2,1,0:T(8,128)(2,1)S(1)}, bf16[8,128,128]{2,1,0:T(8,128)(2,1)}, u32[]{:S(2)}) copy-start(bf16[8,128,128]{2,1,0:T(8,128)(2,1)} %param.11) | copy-start | bytes 786436
  7.2 282.0 %all-reduce.6.cloned.1.call-start = ((), (), s32[]{:S(2)}) async-start(), calls=%async_computation | async-start | bytes 8126464 | tf_op jit(solution)/shard_map/psum | solution.py:109
  10.6 23.6 %collective-permute-start.4 = (bf16[8,8,1,128]{3,2,1,0:T(2,128)(2,1)}, bf16[8,8,1,128]{3,2,1,0:T(2,128)(2,1)S(1)}, u32[]{:S(2)}, u32[]{:S(2)}) collective-permute-start(bf16[8,8,1,128]{3,2,1,0:T(2,128)(2,1)} %get-tuple-element.111), channel_id=1, source_target_pairs={{0,1},{1,2},{2,3},{3,4},{4,5},{5,6},{6,7},{7,8},{8,9},{9,10},{10,1... | collective-permute-start | bytes 49160 | tf_op jit(solution)/shard_map/ppermute | solution.py:29
  15.2 19.0 %collective-permute-start.5 = (bf16[8,8,1,128]{3,2,1,0:T(2,128)(2,1)S(1)}, bf16[8,8,1,128]{3,2,1,0:T(2,128)(2,1)S(1)}, u32[]{:S(2)}, u32[]{:S(2)}) collective-permute-start(bf16[8,8,1,128]{3,2,1,0:T(2,128)(2,1)S(1)} %get-tuple-element.112), channel_id=1, source_target_pairs={{1,0},{2,1},{3,2},{4,3},{5,4},{6,5},{7,6},{8,7},{9,8},{10,9},{11,1... | collective-permute-start | bytes 49160 | tf_op jit(solution)/shard_map/ppermute | solution.py:30
  21.1 9.6 %copy-start.6 = (bf16[27,128,128]{2,1,0:T(8,128)(2,1)S(1)}, bf16[27,128,128]{2,1,0:T(8,128)(2,1)}, u32[]{:S(2)}) copy-start(bf16[27,128,128]{2,1,0:T(8,128)(2,1)} %param.12) | copy-start | bytes 2654212
  22.2 12.9 %collective-permute-start = (bf16[8,8,1,128]{3,2,1,0:T(2,128)(2,1)}, bf16[8,8,1,128]{3,2,1,0:T(2,128)(2,1)S(1)}, u32[]{:S(2)}, u32[]{:S(2)}) collective-permute-start(bf16[8,8,1,128]{3,2,1,0:T(2,128)(2,1)} %get-tuple-element.119), channel_id=1, source_target_pairs={{0,1},{1,2},{2,3},{3,4},{4,5},{5,6},{6,7},{7,8},{8,9},{9,10},{10,1... | collective-permute-start | bytes 49160 | tf_op jit(solution)/shard_map/ppermute | solution.py:29
  25.8 9.2 %collective-permute-start.1 = (bf16[8,8,1,128]{3,2,1,0:T(2,128)(2,1)S(1)}, bf16[8,8,1,128]{3,2,1,0:T(2,128)(2,1)S(1)}, u32[]{:S(2)}, u32[]{:S(2)}) collective-permute-start(bf16[8,8,1,128]{3,2,1,0:T(2,128)(2,1)S(1)} %get-tuple-element.120), channel_id=1, source_target_pairs={{1,0},{2,1},{3,2},{4,3},{5,4},{6,5},{7,6},{8,7},{9,8},{10,9},{11,1... | collective-permute-start | bytes 49160 | tf_op jit(solution)/shard_map/ppermute | solution.py:30
  38.2 1.3 copy-start.8
  38.4 2.2 copy-start.4
  40.7 20.3 %collective-permute-start.6 = (bf16[8,8,1,128]{3,2,1,0:T(2,128)(2,1)S(1)}, bf16[8,8,1,128]{3,2,1,0:T(2,128)(2,1)S(1)}, u32[]{:S(2)}, u32[]{:S(2)}) collective-permute-start(bf16[8,8,1,128]{3,2,1,0:T(2,128)(2,1)S(1)} %get-tuple-element.107), channel_id=1, source_target_pairs={{0,1},{1,2},{2,3},{3,4},{4,5},{5,6},{6,7},{7,8},{8,9},{9,10},{10,1... | collective-permute-start | bytes 49160 | tf_op jit(solution)/shard_map/ppermute | solution.py:29
  44.3 16.6 %collective-permute-start.7 = (bf16[8,8,1,128]{3,2,1,0:T(2,128)(2,1)S(1)}, bf16[8,8,1,128]{3,2,1,0:T(2,128)(2,1)S(1)}, u32[]{:S(2)}, u32[]{:S(2)}) collective-permute-start(bf16[8,8,1,128]{3,2,1,0:T(2,128)(2,1)S(1)} %get-tuple-element.108), channel_id=1, source_target_pairs={{1,0},{2,1},{3,2},{4,3},{5,4},{6,5},{7,6},{8,7},{9,8},{10,9},{11,1... | collective-permute-start | bytes 49160 | tf_op jit(solution)/shard_map/ppermute | solution.py:30
  55.1 7.3 %collective-permute-start.2 = (bf16[8,8,1,128]{3,2,1,0:T(2,128)(2,1)S(1)}, bf16[8,8,1,128]{3,2,1,0:T(2,128)(2,1)S(1)}, u32[]{:S(2)}, u32[]{:S(2)}) collective-permute-start(bf16[8,8,1,128]{3,2,1,0:T(2,128)(2,1)S(1)} %get-tuple-element.115), channel_id=1, source_target_pairs={{0,1},{1,2},{2,3},{3,4},{4,5},{5,6},{6,7},{7,8},{8,9},{9,10},{10,1... | collective-permute-start | bytes 49160 | tf_op jit(solution)/shard_map/ppermute | solution.py:29
  58.8 5.2 %collective-permute-start.3 = (bf16[8,8,1,128]{3,2,1,0:T(2,128)(2,1)S(1)}, bf16[8,8,1,128]{3,2,1,0:T(2,128)(2,1)S(1)}, u32[]{:S(2)}, u32[]{:S(2)}) collective-permute-start(bf16[8,8,1,128]{3,2,1,0:T(2,128)(2,1)S(1)} %get-tuple-element.116), channel_id=1, source_target_pairs={{1,0},{2,1},{3,2},{4,3},{5,4},{6,5},{7,6},{8,7},{9,8},{10,9},{11,1... | collective-permute-start | bytes 49160 | tf_op jit(solution)/shard_map/ppermute | solution.py:30
  66.1 17.9 %copy-start.10 = (bf16[512,3456]{1,0:T(8,128)(2,1)}, bf16[512,3456]{1,0:T(8,128)(2,1)S(1)}, u32[]{:S(2)}) copy-start(bf16[512,3456]{1,0:T(8,128)(2,1)S(1)} %constant_dynamic-update-slice_fusion.94) | copy-start | bytes 10616836
  85.4 23.6 %copy-start.9 = (bf16[8,8,8,128]{3,2,1,0:T(8,128)(2,1)S(1)}, bf16[8,8,8,128]{3,2,1,0:T(8,128)(2,1)}, u32[]{:S(2)}) copy-start(bf16[8,8,8,128]{3,2,1,0:T(8,128)(2,1)} %get-tuple-element.10) | copy-start | bytes 393220
  85.4 25.0 %copy-start.7 = (bf16[27,128,128]{1,2,0:T(8,128)(2,1)S(1)}, bf16[27,128,128]{1,2,0:T(8,128)(2,1)}, u32[]{:S(2)}) copy-start(bf16[27,128,128]{1,2,0:T(8,128)(2,1)} %rev.8) | copy-start | bytes 2654212
  97.7 15.8 %copy-start.3 = (bf16[1024,512]{1,0:T(8,128)(2,1)S(1)}, bf16[1024,512]{1,0:T(8,128)(2,1)}, u32[]{:S(2)}) copy-start(bf16[1024,512]{1,0:T(8,128)(2,1)} %copy.39) | copy-start | bytes 3145732
  107.3 6.6 %copy-start.2 = (bf16[3456,512]{1,0:T(8,128)(2,1)S(1)}, bf16[3456,512]{1,0:T(8,128)(2,1)}, u32[]{:S(2)}) copy-start(bf16[3456,512]{1,0:T(8,128)(2,1)} %copy.38) | copy-start | bytes 10616836
  293.7 5.4 %copy-start.1 = (bf16[32,128,128]{2,1,0:T(8,128)(2,1)S(1)}, bf16[32,128,128]{2,1,0:T(8,128)(2,1)}, u32[]{:S(2)}) copy-start(bf16[32,128,128]{2,1,0:T(8,128)(2,1)} %param.7) | copy-start | bytes 3145732
Sparse Core Ops, SparseCore 0:
  117.5 171.6 all-reduce.5
where the time goes:
time: 307 us; the launch traced here: 306 us
  waiting for transfers between devices  164 us (53%)
  local copies, waits for them, and re-layouts  77.2 us (25%)
  starting transfers between devices  23.4 us (8%)
  between operations  15.7 us (5%)
  matrix products  14 us (5%)
  other arithmetic  11.4 us (4%)
    psum x1, waiting for transfers between devices, on_device(): summed = lax.psum(raw_grads, 'range')  163 us
    unnamed x130, local copies, waits for them, and re-layouts  42.5 us
    ppermute x4, starting transfers between devices, padded(): low = lax.ppermute(grid[:, :, PZ - 1:], 'range', forward)  15.5 us
    ppermute x4, starting transfers between devices, padded(): high = lax.ppermute(grid[:, :, :1], 'range', backward)  7.86 us
  transfers between devices with their start and end apart: 9, of which 2 were waited for; matrix products, arithmetic and copies ran while one was open for 10% of the time, Pallas kernels for 0%

commit v1 on v0

--- a/solution.py
+++ b/solution.py
@@ -41,6 +41,71 @@
         for sz in range(3)
     ]
     return jnp.concatenate(parts, axis=-1).reshape(-1, 27 * channels)
+
+
+AXIS_SHIFT = {"y": 1, "x": 3, "z": 5}
+PART_ORDERS = (("y", "x", "z"), ("x", "z", "y"), ("z", "y", "x"))
+
+
+def coordinate(index, shift):
+    return (index >> shift) & 3
+
+
+def partner(index, shift, stage):
+    c = (index >> shift) & 3
+    other = c ^ 1 if stage == 0 else 3 - c
+    return index + ((other - c) << shift)
+
+
+def keep_bit(c, stage):
+    if stage == 0:
+        return ((c == 1) | (c == 2)).astype(jnp.int32)
+    return (c >= 2).astype(jnp.int32)
+
+
+def exchange_steps(order):
+    return [(AXIS_SHIFT[axis], stage) for axis in order for stage in (0, 1)]
+
+
+def split_halves(y, bit):
+    h = y.shape[0] // 2
+    keep = lax.dynamic_slice_in_dim(y, bit * h, h, 0)
+    send = lax.dynamic_slice_in_dim(y, (1 - bit) * h, h, 0)
+    return keep, send
+
+
+def join_halves(y, got, bit):
+    h = y.shape[0]
+    full = jnp.zeros((2 * h,) + y.shape[1:], y.dtype)
+    full = lax.dynamic_update_slice_in_dim(full, y, bit * h, 0)
+    return lax.dynamic_update_slice_in_dim(full, got, (1 - bit) * h, 0)
+
+
+def torus_psum(flat):
+    count = lax.axis_size("range")
+    index = lax.axis_index("range")
+    core_perm = [(i, i ^ 1) for i in range(count)]
+    core_bit = index & 1
+    keep, send = split_halves(flat, core_bit)
+    y = keep + lax.ppermute(send, "range", core_perm)
+    parts = jnp.split(y, len(PART_ORDERS), 0)
+    reduced = []
+    for part, order in zip(parts, PART_ORDERS):
+        for shift, stage in exchange_steps(order):
+            perm = [(i, partner(i, shift, stage)) for i in range(count)]
+            bit = keep_bit(coordinate(index, shift), stage)
+            keep, send = split_halves(part, bit)
+            part = keep + lax.ppermute(send, "range", perm)
+        reduced.append(part)
+    gathered = []
+    for part, order in zip(reduced, PART_ORDERS):
+        for shift, stage in reversed(exchange_steps(order)):
+            perm = [(i, partner(i, shift, stage)) for i in range(count)]
+            bit = keep_bit(coordinate(index, shift), stage)
+            part = join_halves(part, lax.ppermute(part, "range", perm), bit)
+        gathered.append(part)
+    y = jnp.concatenate(gathered, 0)
+    return join_halves(y, lax.ppermute(y, "range", core_perm), core_bit)
 
 
 def reversed_kernel(weights):
@@ -106,7 +171,10 @@
         0,
     )
     limit = jnp.float32(channels * math.sqrt(62.0))
-    summed = lax.psum(raw_grads, "range")
+    total_values = raw_grads.size
+    rows = 8064
+    flat = jnp.pad(raw_grads.reshape(-1), (0, rows * channels - total_values)).reshape(rows, channels)
+    summed = torus_psum(flat).reshape(-1)[:total_values].reshape(raw_grads.shape)
     grad_total = jnp.sqrt(jnp.sum(summed * summed))
     clipped = summed * jnp.minimum(jnp.float32(1.0), limit / grad_total)
     section_out = from_grid(section.reshape(2 * PX, 2 * PY, PZ, channels))[slot_of]

time: 307 us -> 249 us (0.81)
  waiting for transfers between devices: 164 us -> 25.9 us
  starting transfers between devices: 23.4 us -> 98.2 us
  local copies, waits for them, and re-layouts: 77.2 us -> 92.8 us
  between operations: 15.7 us -> 3.09 us
    psum x1 -> x0, waiting for transfers between devices: 163 us -> none  [on_device(): summed = lax.psum(raw_grads, 'range')]
    ppermute x0 -> x38, starting transfers between devices: none -> 74.8 us  [the longest x18 46.1 us: torus_psum(): part = keep + lax.ppermute(send, 'range', perm)]
    ppermute x0 -> x38, waiting for transfers between devices: none -> 24.3 us  [the longest x18 14.9 us: torus_psum(): part = join_halves(part, lax.ppermute(part, 'range', perm), bit)]
    dynamic_update_slice x0 -> x37, local copies, waits for them, and re-layouts: none -> 8.75 us  [the longest x19 5.49 us: join_halves(): return lax.dynamic_update_slice_in_dim(full, got, (1 - bit) * h, 0)]
    unnamed x130 -> x132, local copies, waits for them, and re-layouts: 42.5 us -> 44.2 us
  transfers between devices with their start and end apart: 9 -> 46, of which waited for: 2 -> 17; matrix products, arithmetic and copies ran while one was open for 10% -> 16% of each run, Pallas kernels for 0% -> 0%
where the time goes in v1:
time: 249 us; the launch traced here: 248 us
  starting transfers between devices  98.2 us (39%)
  local copies, waits for them, and re-layouts  92.8 us (37%)
  waiting for transfers between devices  25.9 us (10%)
  other arithmetic  14.4 us (6%)
  matrix products  14 us (6%)
  between operations  3.09 us (1%)
    ppermute x18, starting transfers between devices, torus_psum(): part = keep + lax.ppermute(send, 'range', perm)  46.1 us
    unnamed x132, local copies, waits for them, and re-layouts  44.2 us
    ppermute x18, starting transfers between devices, torus_psum(): part = join_halves(part, lax.ppermute(part, 'range', perm), bit)  15.6 us
    ppermute x4, starting transfers between devices, padded(): low = lax.ppermute(grid[:, :, PZ - 1:], 'range', forward)  15.5 us
    ppermute x18, waiting for transfers between devices, torus_psum(): part = join_halves(part, lax.ppermute(part, 'range', perm), bit)  14.9 us
    ppermute x1, starting transfers between devices, torus_psum(): return join_halves(y, lax.ppermute(y, 'range', core_perm), core_bit)  13.1 us
    ppermute x4, starting transfers between devices, padded(): high = lax.ppermute(grid[:, :, :1], 'range', backward)  7.86 us
    dot_general x1, local copies, waits for them, and re-layouts, on_device(): lax.dot_general(act_cols, cot_rows, contract_rows, preferred_element_type...  5.84 us
  transfers between devices with their start and end apart: 46, of which 17 were waited for; matrix products, arithmetic and copies ran while one was open for 16% of the time, Pallas kernels for 0%

profile of v1, /device:TPU:1, one launch (start us, length us, event | category | flops | bytes accessed | tf_op | source)
XLA Modules:
  0.0 248.4 jit_solution(14755683659954728979)
XLA Ops:
  3.4 4.6 %collective-permute-start.4 = (bf16[8,8,1,128]{3,2,1,0:T(2,128)(2,1)S(1)}, bf16[8,8,1,128]{3,2,1,0:T(2,128)(2,1)S(1)}, u32[]{:S(2)}, u32[]{:S(2)}) collective-permute-start(bf16[8,8,1,128]{3,2,1,0:T(2,128)(2,1)S(1)} %get-tuple-element.116), channel_id=1, source_target_pairs={{0,1},{1,2},{2,3},{3,4},{4,5},{5,6},{6,7},{7,8},{8,9},{9,10},{10,1... | collective-permute-start | bytes 49160 | tf_op jit(solution)/shard_map/ppermute | solution.py:29
  8.0 1.9 collective-permute-start.5
  15.0 3.6 %collective-permute-start = (bf16[8,8,1,128]{3,2,1,0:T(2,128)(2,1)}, bf16[8,8,1,128]{3,2,1,0:T(2,128)(2,1)S(1)}, u32[]{:S(2)}, u32[]{:S(2)}) collective-permute-start(bf16[8,8,1,128]{3,2,1,0:T(2,128)(2,1)} %get-tuple-element.124), channel_id=1, source_target_pairs={{0,1},{1,2},{2,3},{3,4},{4,5},{5,6},{6,7},{7,8},{8,9},{9,10},{10,1... | collective-permute-start | bytes 49160 | tf_op jit(solution)/shard_map/ppermute | solution.py:29
  33.5 3.6 %collective-permute-start.6 = (bf16[8,8,1,128]{3,2,1,0:T(2,128)(2,1)S(1)}, bf16[8,8,1,128]{3,2,1,0:T(2,128)(2,1)S(1)}, u32[]{:S(2)}, u32[]{:S(2)}) collective-permute-start(bf16[8,8,1,128]{3,2,1,0:T(2,128)(2,1)S(1)} %get-tuple-element.112), channel_id=1, source_target_pairs={{0,1},{1,2},{2,3},{3,4},{4,5},{5,6},{6,7},{7,8},{8,9},{9,10},{10,1... | collective-permute-start | bytes 49160 | tf_op jit(solution)/shard_map/ppermute | solution.py:29
  37.1 1.9 collective-permute-start.7
  39.1 5.7 %copy.37 = bf16[3456,512]{1,0:T(8,128)(2,1)} copy(bf16[3456,512]{0,1:T(8,128)(2,1)} %bitcast.192) | data formatting | bytes 7077888 | tf_op jit(solution)/shard_map/dot_general | solution.py:156
  44.8 3.1 %fusion.15 = f32[27,128,128]{2,1,0:T(8,128)S(1)} fusion(bf16[27,128,512]{2,1,0:T(8,128)(2,1)} %bitcast.180, bf16[512,128]{1,0:T(8,128)(2,1)S(1)} %fusion.2), kind=kOutput, calls=%fused_computation.167 | convolution fusion | flops 452984832 | bytes 5439488 | tf_op jit(solution)/shard_map/dot_general | solution.py:156
  48.0 3.6 %collective-permute-start.2 = (bf16[8,8,1,128]{3,2,1,0:T(2,128)(2,1)S(1)}, bf16[8,8,1,128]{3,2,1,0:T(2,128)(2,1)S(1)}, u32[]{:S(2)}, u32[]{:S(2)}) collective-permute-start(bf16[8,8,1,128]{3,2,1,0:T(2,128)(2,1)S(1)} %get-tuple-element.120), channel_id=1, source_target_pairs={{0,1},{1,2},{2,3},{3,4},{4,5},{5,6},{6,7},{7,8},{8,9},{9,10},{10,1... | collective-permute-start | bytes 49160 | tf_op jit(solution)/shard_map/ppermute | solution.py:29
  51.6 2.1 collective-permute-start.3
  78.0 5.8 %copy.38 = bf16[3456,512]{1,0:T(8,128)(2,1)} copy(bf16[3456,512]{0,1:T(8,128)(2,1)} %bitcast.138) | data formatting | bytes 7077888 | tf_op jit(solution)/shard_map/dot_general | solution.py:157
  103.0 3.1 %fusion.3 = bf16[512,128]{1,0:T(8,128)(2,1)S(1)} fusion(bf16[512,3456]{1,0:T(8,128)(2,1)} %constant_dynamic-update-slice_fusion.81, bf16[3456,128]{1,0:T(8,128)(2,1)S(1)} %bitcast.208, bf16[512,128]{1,0:T(8,128)(2,1)S(1)} %bitcast.190), kind=kOutput, calls=%fused_computation.23 | convolution fusion | flops 453181440 | bytes 4685824 | tf_op jit(solution)/shard_map/dot_general | solution.py:152
  108.2 2.0 copy-done.2
  111.7 4.5 %collective-permute-done.8 = f32[4032,128]{1,0:T(8,128)} collective-permute-done((f32[4032,128]{1,0:T(8,128)}, f32[4032,128]{1,0:T(8,128)}, u32[]{:S(2)}, u32[]{:S(2)}) %collective-permute-start.8) | collective-permute-done | bytes 2064416 | tf_op jit(solution)/shard_map/ppermute | solution.py:90
  116.2 2.4 dynamic-slice_add_fusion
  120.8 7.1 %collective-permute-start.21 = (f32[672,128]{1,0:T(8,128)S(1)}, f32[672,128]{1,0:T(8,128)S(1)}, u32[]{:S(2)}, u32[]{:S(2)}) collective-permute-start(f32[672,128]{1,0:T(8,128)S(1)} %constant_dynamic-slice_fusion.13), channel_id=1, source_target_pairs={{0,8},{1,9},{2,10},{3,11},{4,12},{5,13},{6,14},{7,15},{8,0},{9,1},... | collective-permute-start | bytes 1032200 | tf_op jit(solution)/shard_map/ppermute | solution.py:98
  127.9 9.0 %collective-permute-start.33 = (f32[672,128]{1,0:T(8,128)S(1)}, f32[672,128]{1,0:T(8,128)S(1)}, u32[]{:S(2)}, u32[]{:S(2)}) collective-permute-start(f32[672,128]{1,0:T(8,128)S(1)} %constant_dynamic-slice_fusion.6), channel_id=1, source_target_pairs={{0,32},{1,33},{2,34},{3,35},{4,36},{5,37},{6,38},{7,39},{8,40},{9,... | collective-permute-start | bytes 1032200 | tf_op jit(solution)/shard_map/ppermute | solution.py:98
  137.0 3.1 %collective-permute-start.10 = (f32[336,128]{1,0:T(8,128)S(1)}, f32[336,128]{1,0:T(8,128)S(1)}, u32[]{:S(2)}, u32[]{:S(2)}) collective-permute-start(f32[336,128]{1,0:T(8,128)S(1)} %constant_dynamic-slice_fusion.19), channel_id=1, source_target_pairs={{0,6},{1,7},{2,4},{3,5},{4,2},{5,3},{6,0},{7,1},{8,14},{9,15},{10,... | collective-permute-start | bytes 516104 | tf_op jit(solution)/shard_map/ppermute | solution.py:98
  140.2 11.3 %collective-permute-start.22 = (f32[336,128]{1,0:T(8,128)S(1)}, f32[336,128]{1,0:T(8,128)S(1)}, u32[]{:S(2)}, u32[]{:S(2)}) collective-permute-start(f32[336,128]{1,0:T(8,128)S(1)} %constant_dynamic-slice_fusion.12), channel_id=1, source_target_pairs={{0,24},{1,25},{2,26},{3,27},{4,28},{5,29},{6,30},{7,31},{8,16},{9,... | collective-permute-start | bytes 516104 | tf_op jit(solution)/shard_map/ppermute | solution.py:98
  151.8 3.1 %collective-permute-done.22 = f32[336,128]{1,0:T(8,128)S(1)} collective-permute-done((f32[336,128]{1,0:T(8,128)S(1)}, f32[336,128]{1,0:T(8,128)S(1)}, u32[]{:S(2)}, u32[]{:S(2)}) %collective-permute-start.22) | collective-permute-done | bytes 172064 | tf_op jit(solution)/shard_map/ppermute | solution.py:98
  157.4 2.0 collective-permute-start.12
  159.5 2.0 collective-permute-start.24
  198.5 2.3 collective-permute-done.31
  201.6 3.0 %collective-permute-done.20 = f32[672,128]{1,0:T(8,128)S(1)} collective-permute-done((f32[672,128]{1,0:T(8,128)S(1)}, f32[672,128]{1,0:T(8,128)S(1)}, u32[]{:S(2)}, u32[]{:S(2)}) %collective-permute-start.20) | collective-permute-done | bytes 344096 | tf_op jit(solution)/shard_map/ppermute | solution.py:105
  204.6 2.4 collective-permute-done.32
  208.4 2.3 broadcast_in_dim.29
  210.7 2.3 pad_maximum_fusion.1
  212.9 13.1 %collective-permute-start.45 = (f32[4032,128]{1,0:T(8,128)}, f32[4032,128]{1,0:T(8,128)}, u32[]{:S(2)}, u32[]{:S(2)}) collective-permute-start(f32[4032,128]{1,0:T(8,128)} %get-tuple-element.9), channel_id=1, source_target_pairs={{0,1},{1,0},{2,3},{3,2},{4,5},{5,4},{6,7},{7,6},{8,9},{9,8},{10,11... | collective-permute-start | bytes 6193160 | tf_op jit(solution)/shard_map/ppermute | solution.py:108
  229.2 3.3 %fusion.1 = bf16[512,128]{1,0:T(8,128)(2,1)S(1)} fusion(bf16[512,3456]{1,0:T(8,128)(2,1)} %constant_dynamic-update-slice_fusion.27, bf16[3456,128]{1,0:T(8,128)(2,1)} %bitcast.207, bf16[512,128]{1,0:T(8,128)(2,1)S(1)} %convolution_convert_fusion.1), kind=kOutput, calls=%fused_computation.21 | convolution fusion | flops 453181440 | bytes 4685824 | tf_op jit(solution)/shard_map/dot_general | solution.py:140
  235.5 3.1 %constant_dynamic-update-slice_fusion.108 = f32[8064,128]{1,0:T(8,128)} fusion(f32[8064,128]{1,0:T(8,128)} %get-tuple-element.10, f32[4032,128]{1,0:T(8,128)} %collective-permute-done.45, s32[]{:T(128)S(6)} %select_n.73), kind=kLoop, calls=%fused_computation.180 | loop fusion | bytes 4128772 | tf_op jit(solution)/shard_map/dynamic_update_slice | solution.py:81
  238.5 3.8 %multiply_reduce_fusion = f32[]{:T(128)} fusion(f32[8064,128]{1,0:T(8,128)} %constant_dynamic-update-slice_fusion.108), kind=kLoop, calls=%fused_computation.8 | loop fusion | flops 2031615 | bytes 4063236 | tf_op jit(solution)/shard_map/reduce_sum | solution.py:178
  243.0 2.5 %slice_multiply_fusion = f32[7936,128]{1,0:T(8,128)S(1)} fusion(f32[8064,128]{1,0:T(8,128)} %constant_dynamic-update-slice_fusion.108, f32[]{:T(128)S(6)} %min.3), kind=kLoop, calls=%fused_computation.9 | loop fusion | flops 1015808 | bytes 8126468 | tf_op jit(solution)/shard_map/mul | solution.py:179
  245.5 2.0 fusion.29
  (356 shorter events, 119.5 us)
Async XLA Ops:
  3.4 23.6 %collective-permute-start.4 = (bf16[8,8,1,128]{3,2,1,0:T(2,128)(2,1)S(1)}, bf16[8,8,1,128]{3,2,1,0:T(2,128)(2,1)S(1)}, u32[]{:S(2)}, u32[]{:S(2)}) collective-permute-start(bf16[8,8,1,128]{3,2,1,0:T(2,128)(2,1)S(1)} %get-tuple-element.116), channel_id=1, source_target_pairs={{0,1},{1,2},{2,3},{3,4},{4,5},{5,6},{6,7},{7,8},{8,9},{9,10},{10,1... | collective-permute-start | bytes 49160 | tf_op jit(solution)/shard_map/ppermute | solution.py:29
  8.0 19.0 %collective-permute-start.5 = (bf16[8,8,1,128]{3,2,1,0:T(2,128)(2,1)S(1)}, bf16[8,8,1,128]{3,2,1,0:T(2,128)(2,1)S(1)}, u32[]{:S(2)}, u32[]{:S(2)}) collective-permute-start(bf16[8,8,1,128]{3,2,1,0:T(2,128)(2,1)S(1)} %get-tuple-element.117), channel_id=1, source_target_pairs={{1,0},{2,1},{3,2},{4,3},{5,4},{6,5},{7,6},{8,7},{9,8},{10,9},{11,1... | collective-permute-start | bytes 49160 | tf_op jit(solution)/shard_map/ppermute | solution.py:30
  15.0 12.9 %collective-permute-start = (bf16[8,8,1,128]{3,2,1,0:T(2,128)(2,1)}, bf16[8,8,1,128]{3,2,1,0:T(2,128)(2,1)S(1)}, u32[]{:S(2)}, u32[]{:S(2)}) collective-permute-start(bf16[8,8,1,128]{3,2,1,0:T(2,128)(2,1)} %get-tuple-element.124), channel_id=1, source_target_pairs={{0,1},{1,2},{2,3},{3,4},{4,5},{5,6},{6,7},{7,8},{8,9},{9,10},{10,1... | collective-permute-start | bytes 49160 | tf_op jit(solution)/shard_map/ppermute | solution.py:29
  18.7 9.2 %collective-permute-start.1 = (bf16[8,8,1,128]{3,2,1,0:T(2,128)(2,1)}, bf16[8,8,1,128]{3,2,1,0:T(2,128)(2,1)S(1)}, u32[]{:S(2)}, u32[]{:S(2)}) collective-permute-start(bf16[8,8,1,128]{3,2,1,0:T(2,128)(2,1)} %get-tuple-element.125), channel_id=1, source_target_pairs={{1,0},{2,1},{3,2},{4,3},{5,4},{6,5},{7,6},{8,7},{9,8},{10,9},{11,1... | collective-permute-start | bytes 49160 | tf_op jit(solution)/shard_map/ppermute | solution.py:30
  33.5 20.2 %collective-permute-start.6 = (bf16[8,8,1,128]{3,2,1,0:T(2,128)(2,1)S(1)}, bf16[8,8,1,128]{3,2,1,0:T(2,128)(2,1)S(1)}, u32[]{:S(2)}, u32[]{:S(2)}) collective-permute-start(bf16[8,8,1,128]{3,2,1,0:T(2,128)(2,1)S(1)} %get-tuple-element.112), channel_id=1, source_target_pairs={{0,1},{1,2},{2,3},{3,4},{4,5},{5,6},{6,7},{7,8},{8,9},{9,10},{10,1... | collective-permute-start | bytes 49160 | tf_op jit(solution)/shard_map/ppermute | solution.py:29
  37.1 16.6 %collective-permute-start.7 = (bf16[8,8,1,128]{3,2,1,0:T(2,128)(2,1)S(1)}, bf16[8,8,1,128]{3,2,1,0:T(2,128)(2,1)S(1)}, u32[]{:S(2)}, u32[]{:S(2)}) collective-permute-start(bf16[8,8,1,128]{3,2,1,0:T(2,128)(2,1)S(1)} %get-tuple-element.113), channel_id=1, source_target_pairs={{1,0},{2,1},{3,2},{4,3},{5,4},{6,5},{7,6},{8,7},{9,8},{10,9},{11,1... | collective-permute-start | bytes 49160 | tf_op jit(solution)/shard_map/ppermute | solution.py:30
  48.0 7.3 %collective-permute-start.2 = (bf16[8,8,1,128]{3,2,1,0:T(2,128)(2,1)S(1)}, bf16[8,8,1,128]{3,2,1,0:T(2,128)(2,1)S(1)}, u32[]{:S(2)}, u32[]{:S(2)}) collective-permute-start(bf16[8,8,1,128]{3,2,1,0:T(2,128)(2,1)S(1)} %get-tuple-element.120), channel_id=1, source_target_pairs={{0,1},{1,2},{2,3},{3,4},{4,5},{5,6},{6,7},{7,8},{8,9},{9,10},{10,1... | collective-permute-start | bytes 49160 | tf_op jit(solution)/shard_map/ppermute | solution.py:29
  51.6 5.2 %collective-permute-start.3 = (bf16[8,8,1,128]{3,2,1,0:T(2,128)(2,1)S(1)}, bf16[8,8,1,128]{3,2,1,0:T(2,128)(2,1)S(1)}, u32[]{:S(2)}, u32[]{:S(2)}) collective-permute-start(bf16[8,8,1,128]{3,2,1,0:T(2,128)(2,1)S(1)} %get-tuple-element.121), channel_id=1, source_target_pairs={{1,0},{2,1},{3,2},{4,3},{5,4},{6,5},{7,6},{8,7},{9,8},{10,9},{11,1... | collective-permute-start | bytes 49160 | tf_op jit(solution)/shard_map/ppermute | solution.py:30
  111.7 4.5 %collective-permute-start.8 = (f32[4032,128]{1,0:T(8,128)}, f32[4032,128]{1,0:T(8,128)}, u32[]{:S(2)}, u32[]{:S(2)}) collective-permute-start(f32[4032,128]{1,0:T(8,128)} %constant_dynamic-slice_fusion.21), channel_id=1, source_target_pairs={{0,1},{1,0},{2,3},{3,2},{4,5},{5,4},{6,7},{7,6},{8,9},{9,8},{10,11... | collective-permute-start | bytes 6193160 | tf_op jit(solution)/shard_map/ppermute | solution.py:90
  119.5 17.4 %collective-permute-start.9 = (f32[672,128]{1,0:T(8,128)}, f32[672,128]{1,0:T(8,128)S(1)}, u32[]{:S(2)}, u32[]{:S(2)}) collective-permute-start(f32[672,128]{1,0:T(8,128)} %constant_dynamic-slice_fusion.20), channel_id=1, source_target_pairs={{0,2},{1,3},{2,0},{3,1},{4,6},{5,7},{6,4},{7,5},{8,10},{9,11},{10,... | collective-permute-start | bytes 1032200 | tf_op jit(solution)/shard_map/ppermute | solution.py:98
  120.8 19.3 %collective-permute-start.21 = (f32[672,128]{1,0:T(8,128)S(1)}, f32[672,128]{1,0:T(8,128)S(1)}, u32[]{:S(2)}, u32[]{:S(2)}) collective-permute-start(f32[672,128]{1,0:T(8,128)S(1)} %constant_dynamic-slice_fusion.13), channel_id=1, source_target_pairs={{0,8},{1,9},{2,10},{3,11},{4,12},{5,13},{6,14},{7,15},{8,0},{9,1},... | collective-permute-start | bytes 1032200 | tf_op jit(solution)/shard_map/ppermute | solution.py:98
  127.9 23.6 %collective-permute-start.33 = (f32[672,128]{1,0:T(8,128)S(1)}, f32[672,128]{1,0:T(8,128)S(1)}, u32[]{:S(2)}, u32[]{:S(2)}) collective-permute-start(f32[672,128]{1,0:T(8,128)S(1)} %constant_dynamic-slice_fusion.6), channel_id=1, source_target_pairs={{0,32},{1,33},{2,34},{3,35},{4,36},{5,37},{6,38},{7,39},{8,40},{9,... | collective-permute-start | bytes 1032200 | tf_op jit(solution)/shard_map/ppermute | solution.py:98
  137.0 14.7 %collective-permute-start.10 = (f32[336,128]{1,0:T(8,128)S(1)}, f32[336,128]{1,0:T(8,128)S(1)}, u32[]{:S(2)}, u32[]{:S(2)}) collective-permute-start(f32[336,128]{1,0:T(8,128)S(1)} %constant_dynamic-slice_fusion.19), channel_id=1, source_target_pairs={{0,6},{1,7},{2,4},{3,5},{4,2},{5,3},{6,0},{7,1},{8,14},{9,15},{10,... | collective-permute-start | bytes 516104 | tf_op jit(solution)/shard_map/ppermute | solution.py:98
  140.2 14.8 %collective-permute-start.22 = (f32[336,128]{1,0:T(8,128)S(1)}, f32[336,128]{1,0:T(8,128)S(1)}, u32[]{:S(2)}, u32[]{:S(2)}) collective-permute-start(f32[336,128]{1,0:T(8,128)S(1)} %constant_dynamic-slice_fusion.12), channel_id=1, source_target_pairs={{0,24},{1,25},{2,26},{3,27},{4,28},{5,29},{6,30},{7,31},{8,16},{9,... | collective-permute-start | bytes 516104 | tf_op jit(solution)/shard_map/ppermute | solution.py:98
  151.6 5.5 %collective-permute-start.34 = (f32[336,128]{1,0:T(8,128)S(1)}, f32[336,128]{1,0:T(8,128)S(1)}, u32[]{:S(2)}, u32[]{:S(2)}) collective-permute-start(f32[336,128]{1,0:T(8,128)S(1)} %constant_dynamic-slice_fusion.5), channel_id=1, source_target_pairs={{0,96},{1,97},{2,98},{3,99},{4,100},{5,101},{6,102},{7,103},{8,104... | collective-permute-start | bytes 516104 | tf_op jit(solution)/shard_map/ppermute | solution.py:98
  151.7 5.6 %collective-permute-start.11 = (f32[168,128]{1,0:T(8,128)S(1)}, f32[168,128]{1,0:T(8,128)S(1)}, u32[]{:S(2)}, u32[]{:S(2)}) collective-permute-start(f32[168,128]{1,0:T(8,128)S(1)} %constant_dynamic-slice_fusion.18), channel_id=1, source_target_pairs={{0,8},{1,9},{2,10},{3,11},{4,12},{5,13},{6,14},{7,15},{8,0},{9,1},... | collective-permute-start | bytes 258056 | tf_op jit(solution)/shard_map/ppermute | solution.py:98
  155.0 4.4 %collective-permute-start.23 = (f32[168,128]{1,0:T(8,128)S(1)}, f32[168,128]{1,0:T(8,128)S(1)}, u32[]{:S(2)}, u32[]{:S(2)}) collective-permute-start(f32[168,128]{1,0:T(8,128)S(1)} %constant_dynamic-slice_fusion.11), channel_id=1, source_target_pairs={{0,32},{1,33},{2,34},{3,35},{4,36},{5,37},{6,38},{7,39},{8,40},{9,... | collective-permute-start | bytes 258056 | tf_op jit(solution)/shard_map/ppermute | solution.py:98
  157.4 5.1 %collective-permute-start.12 = (f32[84,128]{1,0:T(8,128)S(1)}, f32[84,128]{1,0:T(8,128)S(1)}, u32[]{:S(2)}, u32[]{:S(2)}) collective-permute-start(f32[84,128]{1,0:T(8,128)S(1)} %constant_dynamic-slice_fusion.17), channel_id=1, source_target_pairs={{0,24},{1,25},{2,26},{3,27},{4,28},{5,29},{6,30},{7,31},{8,16},{9,... | collective-permute-start | bytes 129032 | tf_op jit(solution)/shard_map/ppermute | solution.py:98
  159.5 5.0 %collective-permute-start.24 = (f32[84,128]{1,0:T(8,128)S(1)}, f32[84,128]{1,0:T(8,128)S(1)}, u32[]{:S(2)}, u32[]{:S(2)}) collective-permute-start(f32[84,128]{1,0:T(8,128)S(1)} %constant_dynamic-slice_fusion.10), channel_id=1, source_target_pairs={{0,96},{1,97},{2,98},{3,99},{4,100},{5,101},{6,102},{7,103},{8,104... | collective-permute-start | bytes 129032 | tf_op jit(solution)/shard_map/ppermute | solution.py:98
  167.8 6.1 %collective-permute-start.26 = (f32[21,128]{1,0:T(8,128)S(1)}, f32[21,128]{1,0:T(8,128)S(1)}, u32[]{:S(2)}, u32[]{:S(2)}) collective-permute-start(f32[21,128]{1,0:T(8,128)S(1)} %constant_dynamic-slice_fusion.7), channel_id=1, source_target_pairs={{0,6},{1,7},{2,4},{3,5},{4,2},{5,3},{6,0},{7,1},{8,14},{9,15},{10,... | collective-permute-start | bytes 32264 | tf_op jit(solution)/shard_map/ppermute | solution.py:98
  171.6 7.2 %collective-permute-start.38 = (f32[21,128]{1,0:T(8,128)S(1)}, f32[21,128]{1,0:T(8,128)S(1)}, u32[]{:S(2)}, u32[]{:S(2)}) collective-permute-start(f32[21,128]{1,0:T(8,128)S(1)} %constant_dynamic-slice_fusion), channel_id=1, source_target_pairs={{0,24},{1,25},{2,26},{3,27},{4,28},{5,29},{6,30},{7,31},{8,16},{9,... | collective-permute-start | bytes 32264 | tf_op jit(solution)/shard_map/ppermute | solution.py:98
  173.9 6.2 %collective-permute-start.27 = (f32[21,128]{1,0:T(8,128)S(1)}, f32[21,128]{1,0:T(8,128)S(1)}, u32[]{:S(2)}, u32[]{:S(2)}) collective-permute-start(f32[21,128]{1,0:T(8,128)S(1)} %fusion.20), channel_id=1, source_target_pairs={{0,6},{1,7},{2,4},{3,5},{4,2},{5,3},{6,0},{7,1},{8,14},{9,15},{10,... | collective-permute-start | bytes 32264 | tf_op jit(solution)/shard_map/ppermute | solution.py:105
  177.0 12.1 %collective-permute-start.17 = (f32[84,128]{1,0:T(8,128)S(1)}, f32[84,128]{1,0:T(8,128)S(1)}, u32[]{:S(2)}, u32[]{:S(2)}) collective-permute-start(f32[84,128]{1,0:T(8,128)S(1)} %dynamic_update_slice.117), channel_id=1, source_target_pairs={{0,24},{1,25},{2,26},{3,27},{4,28},{5,29},{6,30},{7,31},{8,16},{9,... | collective-permute-start | bytes 129032 | tf_op jit(solution)/shard_map/ppermute | solution.py:105
  184.4 6.6 %collective-permute-start.29 = (f32[84,128]{1,0:T(8,128)S(1)}, f32[84,128]{1,0:T(8,128)S(1)}, u32[]{:S(2)}, u32[]{:S(2)}) collective-permute-start(f32[84,128]{1,0:T(8,128)S(1)} %dynamic_update_slice.129), channel_id=1, source_target_pairs={{0,96},{1,97},{2,98},{3,99},{4,100},{5,101},{6,102},{7,103},{8,104... | collective-permute-start | bytes 129032 | tf_op jit(solution)/shard_map/ppermute | solution.py:105
  186.9 4.5 %collective-permute-start.41 = (f32[84,128]{1,0:T(8,128)S(1)}, f32[84,128]{1,0:T(8,128)S(1)}, u32[]{:S(2)}, u32[]{:S(2)}) collective-permute-start(f32[84,128]{1,0:T(8,128)S(1)} %dynamic_update_slice.141), channel_id=1, source_target_pairs={{0,6},{1,7},{2,4},{3,5},{4,2},{5,3},{6,0},{7,1},{8,14},{9,15},{10,... | collective-permute-start | bytes 129032 | tf_op jit(solution)/shard_map/ppermute | solution.py:105
  192.8 5.5 %collective-permute-start.19 = (f32[336,128]{1,0:T(8,128)S(1)}, f32[336,128]{1,0:T(8,128)S(1)}, u32[]{:S(2)}, u32[]{:S(2)}) collective-permute-start(f32[336,128]{1,0:T(8,128)S(1)} %constant_dynamic-update-slice_fusion.126), channel_id=1, source_target_pairs={{0,6},{1,7},{2,4},{3,5},{4,2},{5,3},{6,0},{7,1},{8,14},{9,15},{10,... | collective-permute-start | bytes 516104 | tf_op jit(solution)/shard_map/ppermute | solution.py:105
  195.0 5.8 %collective-permute-start.31 = (f32[336,128]{1,0:T(8,128)S(1)}, f32[336,128]{1,0:T(8,128)S(1)}, u32[]{:S(2)}, u32[]{:S(2)}) collective-permute-start(f32[336,128]{1,0:T(8,128)S(1)} %constant_dynamic-update-slice_fusion.120), channel_id=1, source_target_pairs={{0,24},{1,25},{2,26},{3,27},{4,28},{5,29},{6,30},{7,31},{8,16},{9,... | collective-permute-start | bytes 516104 | tf_op jit(solution)/shard_map/ppermute | solution.py:105
  195.5 5.8 %collective-permute-start.43 = (f32[336,128]{1,0:T(8,128)S(1)}, f32[336,128]{1,0:T(8,128)S(1)}, u32[]{:S(2)}, u32[]{:S(2)}) collective-permute-start(f32[336,128]{1,0:T(8,128)S(1)} %constant_dynamic-update-slice_fusion.114), channel_id=1, source_target_pairs={{0,96},{1,97},{2,98},{3,99},{4,100},{5,101},{6,102},{7,103},{8,104... | collective-permute-start | bytes 516104 | tf_op jit(solution)/shard_map/ppermute | solution.py:105
  198.4 6.2 %collective-permute-start.20 = (f32[672,128]{1,0:T(8,128)S(1)}, f32[672,128]{1,0:T(8,128)S(1)}, u32[]{:S(2)}, u32[]{:S(2)}) collective-permute-start(f32[672,128]{1,0:T(8,128)S(1)} %constant_dynamic-update-slice_fusion.124), channel_id=1, source_target_pairs={{0,2},{1,3},{2,0},{3,1},{4,6},{5,7},{6,4},{7,5},{8,10},{9,11},{10,... | collective-permute-start | bytes 1032200 | tf_op jit(solution)/shard_map/ppermute | solution.py:105
  200.8 6.2 %collective-permute-start.32 = (f32[672,128]{1,0:T(8,128)S(1)}, f32[672,128]{1,0:T(8,128)S(1)}, u32[]{:S(2)}, u32[]{:S(2)}) collective-permute-start(f32[672,128]{1,0:T(8,128)S(1)} %constant_dynamic-update-slice_fusion.118), channel_id=1, source_target_pairs={{0,8},{1,9},{2,10},{3,11},{4,12},{5,13},{6,14},{7,15},{8,0},{9,1},... | collective-permute-start | bytes 1032200 | tf_op jit(solution)/shard_map/ppermute | solution.py:105
  201.2 7.1 %collective-permute-start.44 = (f32[672,128]{1,0:T(8,128)S(1)}, f32[672,128]{1,0:T(8,128)S(1)}, u32[]{:S(2)}, u32[]{:S(2)}) collective-permute-start(f32[672,128]{1,0:T(8,128)S(1)} %constant_dynamic-update-slice_fusion.112), channel_id=1, source_target_pairs={{0,32},{1,33},{2,34},{3,35},{4,36},{5,37},{6,38},{7,39},{8,40},{9,... | collective-permute-start | bytes 1032200 | tf_op jit(solution)/shard_map/ppermute | solution.py:105
  212.9 22.5 %collective-permute-start.45 = (f32[4032,128]{1,0:T(8,128)}, f32[4032,128]{1,0:T(8,128)}, u32[]{:S(2)}, u32[]{:S(2)}) collective-permute-start(f32[4032,128]{1,0:T(8,128)} %get-tuple-element.9), channel_id=1, source_target_pairs={{0,1},{1,0},{2,3},{3,2},{4,5},{5,4},{6,7},{7,6},{8,9},{9,8},{10,11... | collective-permute-start | bytes 6193160 | tf_op jit(solution)/shard_map/ppermute | solution.py:108
  (26 other events, 184.2 us)

commit v2 on v1

--- a/solution.py
+++ b/solution.py
@@ -32,16 +32,33 @@
     return jnp.pad(wide, ((1, 1), (1, 1), (0, 0), (0, 0)))
 
 
-def columns(pad):
-    channels = pad.shape[-1]
-    parts = [
-        pad[sx : sx + 2 * PX, sy : sy + 2 * PY, sz : sz + PZ]
+def z_columns(pad):
+    return jnp.concatenate([pad[:, :, sz : sz + PZ] for sz in range(3)], axis=-1)
+
+
+def xy_window(zcols, sx, sy):
+    return zcols[sx : sx + 2 * PX, sy : sy + 2 * PY].reshape(-1, zcols.shape[-1])
+
+
+def conv_apply(zcols, weights):
+    channels = weights.shape[-1]
+    taps = weights.reshape(3, 3, 3 * channels, channels)
+    total = None
+    for sx in range(3):
+        for sy in range(3):
+            term = jnp.dot(xy_window(zcols, sx, sy), taps[sx, sy], preferred_element_type=jnp.float32)
+            total = term if total is None else total + term
+    return total
+
+
+def conv_weight_grad(zcols, upstream):
+    contract_rows = (((0,), (0,)), ((), ()))
+    terms = [
+        lax.dot_general(xy_window(zcols, sx, sy), upstream, contract_rows, preferred_element_type=jnp.float32)
         for sx in range(3)
         for sy in range(3)
-        for sz in range(3)
     ]
-    return jnp.concatenate(parts, axis=-1).reshape(-1, 27 * channels)
-
+    return jnp.concatenate(terms, 0)
 
 AXIS_SHIFT = {"y": 1, "x": 3, "z": 5}
 PART_ORDERS = (("y", "x", "z"), ("x", "z", "y"), ("z", "y", "x"))
@@ -99,13 +116,14 @@
         reduced.append(part)
     gathered = []
     for part, order in zip(reduced, PART_ORDERS):
+        part = part.astype(jnp.bfloat16)
         for shift, stage in reversed(exchange_steps(order)):
             perm = [(i, partner(i, shift, stage)) for i in range(count)]
             bit = keep_bit(coordinate(index, shift), stage)
             part = join_halves(part, lax.ppermute(part, "range", perm), bit)
         gathered.append(part)
     y = jnp.concatenate(gathered, 0)
-    return join_halves(y, lax.ppermute(y, "range", core_perm), core_bit)
+    return join_halves(y, lax.ppermute(y, "range", core_perm), core_bit).astype(jnp.float32)
 
 
 def reversed_kernel(weights):
@@ -132,29 +150,29 @@
     hidden = jnp.dot(patches, down_flat, preferred_element_type=f32).astype(bf16)
     hidden_grid = hidden.reshape(2 * PX, 2 * PY, PZ, channels)
 
-    hidden_cols = columns(padded(hidden_grid))
-    pre_act = jnp.dot(hidden_cols, first_w.reshape(-1, channels), preferred_element_type=f32)
+    hidden_cols = z_columns(padded(hidden_grid))
+    pre_act = conv_apply(hidden_cols, first_w)
     activated = jax.nn.silu(pre_act).astype(bf16)
-    act_cols = columns(padded(activated.reshape(2 * PX, 2 * PY, PZ, channels)))
+    act_cols = z_columns(padded(activated.reshape(2 * PX, 2 * PY, PZ, channels)))
     section = (
-        hidden.astype(f32) + jnp.dot(act_cols, second_w.reshape(-1, channels), preferred_element_type=f32)
+        hidden.astype(f32) + conv_apply(act_cols, second_w)
     ).astype(bf16)
 
     cot_grid = to_grid(cotangent[block_at])
     cot_rows = cot_grid.reshape(-1, channels)
-    cot_cols = columns(padded(cot_grid))
-    back_act = jnp.dot(cot_cols, reversed_kernel(second_w).reshape(-1, channels), preferred_element_type=f32)
+    cot_cols = z_columns(padded(cot_grid))
+    back_act = conv_apply(cot_cols, reversed_kernel(second_w))
     sigmoid_pre = jax.nn.sigmoid(pre_act)
     d_pre = (back_act * sigmoid_pre * (1.0 + pre_act * (1.0 - sigmoid_pre))).astype(bf16)
-    d_pre_cols = columns(padded(d_pre.reshape(2 * PX, 2 * PY, PZ, channels)))
+    d_pre_cols = z_columns(padded(d_pre.reshape(2 * PX, 2 * PY, PZ, channels)))
     d_hidden = (
         cot_rows.astype(f32)
-        + jnp.dot(d_pre_cols, reversed_kernel(first_w).reshape(-1, channels), preferred_element_type=f32)
+        + conv_apply(d_pre_cols, reversed_kernel(first_w))
     ).astype(bf16)
 
     contract_rows = (((0,), (0,)), ((), ()))
-    raw_first = lax.dot_general(hidden_cols, d_pre, contract_rows, preferred_element_type=f32)
-    raw_second = lax.dot_general(act_cols, cot_rows, contract_rows, preferred_element_type=f32)
+    raw_first = conv_weight_grad(hidden_cols, d_pre)
+    raw_second = conv_weight_grad(act_cols, cot_rows)
     raw_down = lax.dot_general(patches, d_hidden, contract_rows, preferred_element_type=f32)
 
     back = jnp.dot(d_hidden, down_flat.T, preferred_element_type=f32).astype(bf16)

time: 249 us -> 186 us (0.75)
  local copies, waits for them, and re-layouts: 92.8 us -> 35.2 us
  matrix products: 14 us -> 27 us
  waiting for transfers between devices: 25.9 us -> 15.2 us
  other arithmetic: 14.4 us -> 8.27 us
    unnamed x132 -> x62, local copies, waits for them, and re-layouts: 44.2 us -> 5.42 us
    dot_general x6 -> x54, matrix products: 12.7 us -> 24.7 us  [the longest x36 19.1 us: conv_apply(): jnp.dot(xy_window(zcols, sx, sy), taps[sx, sy], preferred_element_type=jn...]
    dot_general x2 -> x0, local copies, waits for them, and re-layouts: 11.6 us -> none  [the longest x1 5.84 us: on_device(): lax.dot_general(act_cols, cot_rows, contract_rows, preferred_element_type...]
    ppermute x18, waiting for transfers between devices: 14.9 us -> 7.01 us  [torus_psum(): part = join_halves(part, lax.ppermute(part, 'range', perm), bit)]
    ppermute x1, waiting for transfers between devices: 4.45 us -> 0.98 us  [torus_psum(): y = keep + lax.ppermute(send, 'range', core_perm)]
  transfers between devices with their start and end apart: 46 -> 46, of which waited for: 17 -> 13; matrix products, arithmetic and copies ran while one was open for 16% -> 21% of each run, Pallas kernels for 0% -> 0%
where the time goes in v2:
time: 186 us; the launch traced here: 185 us
  starting transfers between devices  96.1 us (52%)
  local copies, waits for them, and re-layouts  35.2 us (19%)
  matrix products  27 us (15%)
  waiting for transfers between devices  15.2 us (8%)
  other arithmetic  8.27 us (4%)
  between operations  3.22 us (2%)
    ppermute x18, starting transfers between devices, torus_psum(): part = keep + lax.ppermute(send, 'range', perm)  45.1 us
    dot_general x36, matrix products, conv_apply(): jnp.dot(xy_window(zcols, sx, sy), taps[sx, sy], preferred_element_type=jn...  19.1 us
    ppermute x18, starting transfers between devices, torus_psum(): part = join_halves(part, lax.ppermute(part, 'range', perm), bit)  16 us
    ppermute x4, starting transfers between devices, padded(): low = lax.ppermute(grid[:, :, PZ - 1:], 'range', forward)  15.5 us
    ppermute x1, starting transfers between devices, torus_psum(): lax.ppermute(y, 'range', core_perm)  11.7 us
    ppermute x4, starting transfers between devices, padded(): high = lax.ppermute(grid[:, :, :1], 'range', backward)  7.86 us
    ppermute x18, waiting for transfers between devices, torus_psum(): part = join_halves(part, lax.ppermute(part, 'range', perm), bit)  7.01 us
    dot_general x18, matrix products, conv_weight_grad(): lax.dot_general(xy_window(zcols, sx, sy), upstream, contract_rows, prefer...  5.61 us
  transfers between devices with their start and end apart: 46, of which 13 were waited for; matrix products, arithmetic and copies ran while one was open for 21% of the time, Pallas kernels for 0%

profile of v2, /device:TPU:1, one launch (start us, length us, event | category | flops | bytes accessed | tf_op | source)
XLA Modules:
  0.0 185.1 jit_solution(1891471395339373686)
XLA Ops:
  4.0 4.6 %collective-permute-start.4 = (bf16[8,8,1,128]{3,2,1,0:T(2,128)(2,1)}, bf16[8,8,1,128]{3,2,1,0:T(2,128)(2,1)}, u32[]{:S(2)}, u32[]{:S(2)}) collective-permute-start(bf16[8,8,1,128]{3,2,1,0:T(2,128)(2,1)} %get-tuple-element.64), channel_id=1, source_target_pairs={{0,1},{1,2},{2,3},{3,4},{4,5},{5,6},{6,7},{7,8},{8,9},{9,10},{10,1... | collective-permute-start | bytes 49160 | tf_op jit(solution)/shard_map/ppermute | solution.py:29
  8.6 1.9 %collective-permute-start.5 = (bf16[8,8,1,128]{3,2,1,0:T(2,128)(2,1)}, bf16[8,8,1,128]{3,2,1,0:T(2,128)(2,1)}, u32[]{:S(2)}, u32[]{:S(2)}) collective-permute-start(bf16[8,8,1,128]{3,2,1,0:T(2,128)(2,1)} %get-tuple-element.65), channel_id=1, source_target_pairs={{1,0},{2,1},{3,2},{4,3},{5,4},{6,5},{7,6},{8,7},{9,8},{10,9},{11,1... | collective-permute-start | bytes 49160 | tf_op jit(solution)/shard_map/ppermute | solution.py:30
  15.0 3.6 %collective-permute-start = (bf16[8,8,1,128]{3,2,1,0:T(2,128)(2,1)S(1)}, bf16[8,8,1,128]{3,2,1,0:T(2,128)(2,1)S(1)}, u32[]{:S(2)}, u32[]{:S(2)}) collective-permute-start(bf16[8,8,1,128]{3,2,1,0:T(2,128)(2,1)S(1)} %get-tuple-element.68), channel_id=1, source_target_pairs={{0,1},{1,2},{2,3},{3,4},{4,5},{5,6},{6,7},{7,8},{8,9},{9,10},{10,1... | collective-permute-start | bytes 49160 | tf_op jit(solution)/shard_map/ppermute | solution.py:29
  18.7 1.9 %collective-permute-start.1 = (bf16[8,8,1,128]{3,2,1,0:T(2,128)(2,1)S(1)}, bf16[8,8,1,128]{3,2,1,0:T(2,128)(2,1)S(1)}, u32[]{:S(2)}, u32[]{:S(2)}) collective-permute-start(bf16[8,8,1,128]{3,2,1,0:T(2,128)(2,1)S(1)} %get-tuple-element.69), channel_id=1, source_target_pairs={{1,0},{2,1},{3,2},{4,3},{5,4},{6,5},{7,6},{8,7},{9,8},{10,9},{11,1... | collective-permute-start | bytes 49160 | tf_op jit(solution)/shard_map/ppermute | solution.py:30
  37.3 3.6 %collective-permute-start.2 = (bf16[8,8,1,128]{3,2,1,0:T(2,128)(2,1)S(1)}, bf16[8,8,1,128]{3,2,1,0:T(2,128)(2,1)S(1)}, u32[]{:S(2)}, u32[]{:S(2)}) collective-permute-start(bf16[8,8,1,128]{3,2,1,0:T(2,128)(2,1)S(1)} %get-tuple-element.66), channel_id=1, source_target_pairs={{0,1},{1,2},{2,3},{3,4},{4,5},{5,6},{6,7},{7,8},{8,9},{9,10},{10,1... | collective-permute-start | bytes 49160 | tf_op jit(solution)/shard_map/ppermute | solution.py:29
  40.9 1.9 %collective-permute-start.3 = (bf16[8,8,1,128]{3,2,1,0:T(2,128)(2,1)S(1)}, bf16[8,8,1,128]{3,2,1,0:T(2,128)(2,1)S(1)}, u32[]{:S(2)}, u32[]{:S(2)}) collective-permute-start(bf16[8,8,1,128]{3,2,1,0:T(2,128)(2,1)S(1)} %get-tuple-element.67), channel_id=1, source_target_pairs={{1,0},{2,1},{3,2},{4,3},{5,4},{6,5},{7,6},{8,7},{9,8},{10,9},{11,1... | collective-permute-start | bytes 49160 | tf_op jit(solution)/shard_map/ppermute | solution.py:30
  42.9 3.6 %collective-permute-start.6 = (bf16[8,8,1,128]{3,2,1,0:T(2,128)(2,1)S(1)}, bf16[8,8,1,128]{3,2,1,0:T(2,128)(2,1)S(1)}, u32[]{:S(2)}, u32[]{:S(2)}) collective-permute-start(bf16[8,8,1,128]{3,2,1,0:T(2,128)(2,1)S(1)} %get-tuple-element.62), channel_id=1, source_target_pairs={{0,1},{1,2},{2,3},{3,4},{4,5},{5,6},{6,7},{7,8},{8,9},{9,10},{10,1... | collective-permute-start | bytes 49160 | tf_op jit(solution)/shard_map/ppermute | solution.py:29
  46.6 2.1 %collective-permute-start.7 = (bf16[8,8,1,128]{3,2,1,0:T(2,128)(2,1)S(1)}, bf16[8,8,1,128]{3,2,1,0:T(2,128)(2,1)S(1)}, u32[]{:S(2)}, u32[]{:S(2)}) collective-permute-start(bf16[8,8,1,128]{3,2,1,0:T(2,128)(2,1)S(1)} %get-tuple-element.63), channel_id=1, source_target_pairs={{1,0},{2,1},{3,2},{4,3},{5,4},{6,5},{7,6},{8,7},{9,8},{10,9},{11,1... | collective-permute-start | bytes 49160 | tf_op jit(solution)/shard_map/ppermute | solution.py:30
  49.5 2.3 %collective-permute-done.7 = bf16[8,8,1,128]{3,2,1,0:T(2,128)(2,1)S(1)} collective-permute-done((bf16[8,8,1,128]{3,2,1,0:T(2,128)(2,1)S(1)}, bf16[8,8,1,128]{3,2,1,0:T(2,128)(2,1)S(1)}, u32[]{:S(2)}, u32[]{:S(2)}) %collective-permute-start.7) | collective-permute-done | bytes 16416 | tf_op jit(solution)/shard_map/ppermute | solution.py:30
  66.2 1.8 dynamic-slice_add_fusion
  70.8 7.6 %collective-permute-start.21 = (f32[672,128]{1,0:T(8,128)S(1)}, f32[672,128]{1,0:T(8,128)S(1)}, u32[]{:S(2)}, u32[]{:S(2)}) collective-permute-start(f32[672,128]{1,0:T(8,128)S(1)} %constant_dynamic-slice_fusion.13), channel_id=1, source_target_pairs={{0,8},{1,9},{2,10},{3,11},{4,12},{5,13},{6,14},{7,15},{8,0},{9,1},... | collective-permute-start | bytes 1032200 | tf_op jit(solution)/shard_map/ppermute | solution.py:115
  78.4 9.0 %collective-permute-start.33 = (f32[672,128]{1,0:T(8,128)S(1)}, f32[672,128]{1,0:T(8,128)S(1)}, u32[]{:S(2)}, u32[]{:S(2)}) collective-permute-start(f32[672,128]{1,0:T(8,128)S(1)} %constant_dynamic-slice_fusion.6), channel_id=1, source_target_pairs={{0,32},{1,33},{2,34},{3,35},{4,36},{5,37},{6,38},{7,39},{8,40},{9,... | collective-permute-start | bytes 1032200 | tf_op jit(solution)/shard_map/ppermute | solution.py:115
  88.8 11.3 %collective-permute-start.22 = (f32[336,128]{1,0:T(8,128)S(1)}, f32[336,128]{1,0:T(8,128)S(1)}, u32[]{:S(2)}, u32[]{:S(2)}) collective-permute-start(f32[336,128]{1,0:T(8,128)S(1)} %constant_dynamic-slice_fusion.12), channel_id=1, source_target_pairs={{0,24},{1,25},{2,26},{3,27},{4,28},{5,29},{6,30},{7,31},{8,16},{9,... | collective-permute-start | bytes 516104 | tf_op jit(solution)/shard_map/ppermute | solution.py:115
  100.4 3.1 %collective-permute-done.22 = f32[336,128]{1,0:T(8,128)S(1)} collective-permute-done((f32[336,128]{1,0:T(8,128)S(1)}, f32[336,128]{1,0:T(8,128)S(1)}, u32[]{:S(2)}, u32[]{:S(2)}) %collective-permute-start.22) | collective-permute-done | bytes 172064 | tf_op jit(solution)/shard_map/ppermute | solution.py:115
  103.6 1.7 collective-permute-start.23
  106.0 2.0 %collective-permute-start.12 = (f32[84,128]{1,0:T(8,128)S(1)}, f32[84,128]{1,0:T(8,128)S(1)}, u32[]{:S(2)}, u32[]{:S(2)}) collective-permute-start(f32[84,128]{1,0:T(8,128)S(1)} %constant_dynamic-slice_fusion.17), channel_id=1, source_target_pairs={{0,24},{1,25},{2,26},{3,27},{4,28},{5,29},{6,30},{7,31},{8,16},{9,... | collective-permute-start | bytes 129032 | tf_op jit(solution)/shard_map/ppermute | solution.py:115
  108.1 2.0 %collective-permute-start.24 = (f32[84,128]{1,0:T(8,128)S(1)}, f32[84,128]{1,0:T(8,128)S(1)}, u32[]{:S(2)}, u32[]{:S(2)}) collective-permute-start(f32[84,128]{1,0:T(8,128)S(1)} %constant_dynamic-slice_fusion.10), channel_id=1, source_target_pairs={{0,96},{1,97},{2,98},{3,99},{4,100},{5,101},{6,102},{7,103},{8,104... | collective-permute-start | bytes 129032 | tf_op jit(solution)/shard_map/ppermute | solution.py:115
  110.2 2.4 %collective-permute-start.36 = (f32[84,128]{1,0:T(8,128)S(1)}, f32[84,128]{1,0:T(8,128)S(1)}, u32[]{:S(2)}, u32[]{:S(2)}) collective-permute-start(f32[84,128]{1,0:T(8,128)S(1)} %constant_dynamic-slice_fusion.3), channel_id=1, source_target_pairs={{0,6},{1,7},{2,4},{3,5},{4,2},{5,3},{6,0},{7,1},{8,14},{9,15},{10,... | collective-permute-start | bytes 129032 | tf_op jit(solution)/shard_map/ppermute | solution.py:115
  116.6 2.2 %collective-permute-start.26 = (f32[21,128]{1,0:T(8,128)S(1)}, f32[21,128]{1,0:T(8,128)S(1)}, u32[]{:S(2)}, u32[]{:S(2)}) collective-permute-start(f32[21,128]{1,0:T(8,128)S(1)} %constant_dynamic-slice_fusion.7), channel_id=1, source_target_pairs={{0,6},{1,7},{2,4},{3,5},{4,2},{5,3},{6,0},{7,1},{8,14},{9,15},{10,... | collective-permute-start | bytes 32264 | tf_op jit(solution)/shard_map/ppermute | solution.py:115
  123.2 1.5 collective-permute-start.39
  129.5 1.9 %convolution_add_fusion.21 = f32[512,128]{1,0:T(8,128)} fusion(f32[512,128]{1,0:T(8,128)S(1)} %convolution_add_fusion.22, bf16[512,384]{1,0:T(8,128)(2,1)S(1)} %bitcast.305, bf16[3,3,384,128]{3,2,1,0:T(8,128)(2,1)} %bitcast.331), kind=kOutput, calls=%fused_computation.59 | convolution fusion | flops 50397184 | bytes 1015808 | tf_op jit(solution)/shard_map/dot_general | solution.py:49
  134.2 1.7 collective-permute-start.41
  140.9 1.6 collective-permute-start.31
  145.7 1.5 collective-permute-done.43
  149.9 1.7 collective-permute-done.44
  153.0 11.7 %collective-permute-start.45 = (bf16[4032,128]{1,0:T(8,128)(2,1)}, bf16[4032,128]{1,0:T(8,128)(2,1)}, u32[]{:S(2)}, u32[]{:S(2)}) collective-permute-start(bf16[4032,128]{1,0:T(8,128)(2,1)} %get-tuple-element.12), channel_id=1, source_target_pairs={{0,1},{1,0},{2,3},{3,2},{4,5},{5,4},{6,7},{7,6},{8,9},{9,8},{10,11... | collective-permute-start | bytes 3096584 | tf_op jit(solution)/shard_map/ppermute | solution.py:126
  164.7 1.9 %convolution_add_fusion.20 = f32[512,128]{1,0:T(8,128)} fusion(f32[512,128]{1,0:T(8,128)S(1)} %copy-done.27, bf16[512,384]{1,0:T(8,128)(2,1)S(1)} %bitcast.303, bf16[3,3,384,128]{3,2,1,0:T(8,128)(2,1)} %bitcast.332), kind=kOutput, calls=%fused_computation.58 | convolution fusion | flops 50397184 | bytes 1015808 | tf_op jit(solution)/shard_map/dot_general | solution.py:49
  166.6 1.5 reshape.320
  168.2 2.4 %copy.31 = bf16[2,2,2,2,2,2,2,4,2,2,2,128]{11,10,7,9,5,8,2,6,4,1,3,0:T(2,128)(2,1)S(1)} copy(bf16[2,2,2,2,2,2,2,4,2,2,2,128]{11,10,9,8,7,6,5,4,3,2,1,0:T(2,128)(2,1)} %reshape.320) | data formatting | bytes 2097152 | tf_op jit(solution)/shard_map/reshape | solution.py:179
  175.4 1.7 gather_fusion.4
  179.6 1.6 fusion
  182.2 2.0 %fusion.38 = (f32[3456,128]{1,0:T(8,128)}, f32[3456,128]{1,0:T(8,128)}) fusion(f32[7936,128]{1,0:T(8,128)S(1)} %convert_multiply_fusion), kind=kLoop, calls=%fused_computation.224 | loop fusion | bytes 7077888 | tf_op jit(solution)/shard_map/slice | solution.py:199
  (328 shorter events, 80.3 us)
Async XLA Ops:
  4.0 22.2 %collective-permute-start.4 = (bf16[8,8,1,128]{3,2,1,0:T(2,128)(2,1)}, bf16[8,8,1,128]{3,2,1,0:T(2,128)(2,1)}, u32[]{:S(2)}, u32[]{:S(2)}) collective-permute-start(bf16[8,8,1,128]{3,2,1,0:T(2,128)(2,1)} %get-tuple-element.64), channel_id=1, source_target_pairs={{0,1},{1,2},{2,3},{3,4},{4,5},{5,6},{6,7},{7,8},{8,9},{9,10},{10,1... | collective-permute-start | bytes 49160 | tf_op jit(solution)/shard_map/ppermute | solution.py:29
  8.6 17.7 %collective-permute-start.5 = (bf16[8,8,1,128]{3,2,1,0:T(2,128)(2,1)}, bf16[8,8,1,128]{3,2,1,0:T(2,128)(2,1)}, u32[]{:S(2)}, u32[]{:S(2)}) collective-permute-start(bf16[8,8,1,128]{3,2,1,0:T(2,128)(2,1)} %get-tuple-element.65), channel_id=1, source_target_pairs={{1,0},{2,1},{3,2},{4,3},{5,4},{6,5},{7,6},{8,7},{9,8},{10,9},{11,1... | collective-permute-start | bytes 49160 | tf_op jit(solution)/shard_map/ppermute | solution.py:30
  15.0 12.8 %collective-permute-start = (bf16[8,8,1,128]{3,2,1,0:T(2,128)(2,1)S(1)}, bf16[8,8,1,128]{3,2,1,0:T(2,128)(2,1)S(1)}, u32[]{:S(2)}, u32[]{:S(2)}) collective-permute-start(bf16[8,8,1,128]{3,2,1,0:T(2,128)(2,1)S(1)} %get-tuple-element.68), channel_id=1, source_target_pairs={{0,1},{1,2},{2,3},{3,4},{4,5},{5,6},{6,7},{7,8},{8,9},{9,10},{10,1... | collective-permute-start | bytes 49160 | tf_op jit(solution)/shard_map/ppermute | solution.py:29
  18.7 9.2 %collective-permute-start.1 = (bf16[8,8,1,128]{3,2,1,0:T(2,128)(2,1)S(1)}, bf16[8,8,1,128]{3,2,1,0:T(2,128)(2,1)S(1)}, u32[]{:S(2)}, u32[]{:S(2)}) collective-permute-start(bf16[8,8,1,128]{3,2,1,0:T(2,128)(2,1)S(1)} %get-tuple-element.69), channel_id=1, source_target_pairs={{1,0},{2,1},{3,2},{4,3},{5,4},{6,5},{7,6},{8,7},{9,8},{10,9},{11,1... | collective-permute-start | bytes 49160 | tf_op jit(solution)/shard_map/ppermute | solution.py:30
  37.3 11.4 %collective-permute-start.2 = (bf16[8,8,1,128]{3,2,1,0:T(2,128)(2,1)S(1)}, bf16[8,8,1,128]{3,2,1,0:T(2,128)(2,1)S(1)}, u32[]{:S(2)}, u32[]{:S(2)}) collective-permute-start(bf16[8,8,1,128]{3,2,1,0:T(2,128)(2,1)S(1)} %get-tuple-element.66), channel_id=1, source_target_pairs={{0,1},{1,2},{2,3},{3,4},{4,5},{5,6},{6,7},{7,8},{8,9},{9,10},{10,1... | collective-permute-start | bytes 49160 | tf_op jit(solution)/shard_map/ppermute | solution.py:29
  40.9 7.8 %collective-permute-start.3 = (bf16[8,8,1,128]{3,2,1,0:T(2,128)(2,1)S(1)}, bf16[8,8,1,128]{3,2,1,0:T(2,128)(2,1)S(1)}, u32[]{:S(2)}, u32[]{:S(2)}) collective-permute-start(bf16[8,8,1,128]{3,2,1,0:T(2,128)(2,1)S(1)} %get-tuple-element.67), channel_id=1, source_target_pairs={{1,0},{2,1},{3,2},{4,3},{5,4},{6,5},{7,6},{8,7},{9,8},{10,9},{11,1... | collective-permute-start | bytes 49160 | tf_op jit(solution)/shard_map/ppermute | solution.py:30
  42.9 6.6 %collective-permute-start.6 = (bf16[8,8,1,128]{3,2,1,0:T(2,128)(2,1)S(1)}, bf16[8,8,1,128]{3,2,1,0:T(2,128)(2,1)S(1)}, u32[]{:S(2)}, u32[]{:S(2)}) collective-permute-start(bf16[8,8,1,128]{3,2,1,0:T(2,128)(2,1)S(1)} %get-tuple-element.62), channel_id=1, source_target_pairs={{0,1},{1,2},{2,3},{3,4},{4,5},{5,6},{6,7},{7,8},{8,9},{9,10},{10,1... | collective-permute-start | bytes 49160 | tf_op jit(solution)/shard_map/ppermute | solution.py:29
  46.6 5.2 %collective-permute-start.7 = (bf16[8,8,1,128]{3,2,1,0:T(2,128)(2,1)S(1)}, bf16[8,8,1,128]{3,2,1,0:T(2,128)(2,1)S(1)}, u32[]{:S(2)}, u32[]{:S(2)}) collective-permute-start(bf16[8,8,1,128]{3,2,1,0:T(2,128)(2,1)S(1)} %get-tuple-element.63), channel_id=1, source_target_pairs={{1,0},{2,1},{3,2},{4,3},{5,4},{6,5},{7,6},{8,7},{9,8},{10,9},{11,1... | collective-permute-start | bytes 49160 | tf_op jit(solution)/shard_map/ppermute | solution.py:30
  68.2 19.2 %collective-permute-start.9 = (f32[672,128]{1,0:T(8,128)S(1)}, f32[672,128]{1,0:T(8,128)S(1)}, u32[]{:S(2)}, u32[]{:S(2)}) collective-permute-start(f32[672,128]{1,0:T(8,128)S(1)} %constant_dynamic-slice_fusion.20), channel_id=1, source_target_pairs={{0,2},{1,3},{2,0},{3,1},{4,6},{5,7},{6,4},{7,5},{8,10},{9,11},{10,... | collective-permute-start | bytes 1032200 | tf_op jit(solution)/shard_map/ppermute | solution.py:115
  70.8 17.9 %collective-permute-start.21 = (f32[672,128]{1,0:T(8,128)S(1)}, f32[672,128]{1,0:T(8,128)S(1)}, u32[]{:S(2)}, u32[]{:S(2)}) collective-permute-start(f32[672,128]{1,0:T(8,128)S(1)} %constant_dynamic-slice_fusion.13), channel_id=1, source_target_pairs={{0,8},{1,9},{2,10},{3,11},{4,12},{5,13},{6,14},{7,15},{8,0},{9,1},... | collective-permute-start | bytes 1032200 | tf_op jit(solution)/shard_map/ppermute | solution.py:115
  78.4 21.7 %collective-permute-start.33 = (f32[672,128]{1,0:T(8,128)S(1)}, f32[672,128]{1,0:T(8,128)S(1)}, u32[]{:S(2)}, u32[]{:S(2)}) collective-permute-start(f32[672,128]{1,0:T(8,128)S(1)} %constant_dynamic-slice_fusion.6), channel_id=1, source_target_pairs={{0,32},{1,33},{2,34},{3,35},{4,36},{5,37},{6,38},{7,39},{8,40},{9,... | collective-permute-start | bytes 1032200 | tf_op jit(solution)/shard_map/ppermute | solution.py:115
  87.5 12.8 %collective-permute-start.10 = (f32[336,128]{1,0:T(8,128)S(1)}, f32[336,128]{1,0:T(8,128)S(1)}, u32[]{:S(2)}, u32[]{:S(2)}) collective-permute-start(f32[336,128]{1,0:T(8,128)S(1)} %constant_dynamic-slice_fusion.19), channel_id=1, source_target_pairs={{0,6},{1,7},{2,4},{3,5},{4,2},{5,3},{6,0},{7,1},{8,14},{9,15},{10,... | collective-permute-start | bytes 516104 | tf_op jit(solution)/shard_map/ppermute | solution.py:115
  88.8 14.8 %collective-permute-start.22 = (f32[336,128]{1,0:T(8,128)S(1)}, f32[336,128]{1,0:T(8,128)S(1)}, u32[]{:S(2)}, u32[]{:S(2)}) collective-permute-start(f32[336,128]{1,0:T(8,128)S(1)} %constant_dynamic-slice_fusion.12), channel_id=1, source_target_pairs={{0,24},{1,25},{2,26},{3,27},{4,28},{5,29},{6,30},{7,31},{8,16},{9,... | collective-permute-start | bytes 516104 | tf_op jit(solution)/shard_map/ppermute | solution.py:115
  100.2 5.5 %collective-permute-start.34 = (f32[336,128]{1,0:T(8,128)S(1)}, f32[336,128]{1,0:T(8,128)S(1)}, u32[]{:S(2)}, u32[]{:S(2)}) collective-permute-start(f32[336,128]{1,0:T(8,128)S(1)} %constant_dynamic-slice_fusion.5), channel_id=1, source_target_pairs={{0,96},{1,97},{2,98},{3,99},{4,100},{5,101},{6,102},{7,103},{8,104... | collective-permute-start | bytes 516104 | tf_op jit(solution)/shard_map/ppermute | solution.py:115
  100.4 5.6 %collective-permute-start.11 = (f32[168,128]{1,0:T(8,128)S(1)}, f32[168,128]{1,0:T(8,128)S(1)}, u32[]{:S(2)}, u32[]{:S(2)}) collective-permute-start(f32[168,128]{1,0:T(8,128)S(1)} %constant_dynamic-slice_fusion.18), channel_id=1, source_target_pairs={{0,8},{1,9},{2,10},{3,11},{4,12},{5,13},{6,14},{7,15},{8,0},{9,1},... | collective-permute-start | bytes 258056 | tf_op jit(solution)/shard_map/ppermute | solution.py:115
  103.6 4.4 %collective-permute-start.23 = (f32[168,128]{1,0:T(8,128)S(1)}, f32[168,128]{1,0:T(8,128)S(1)}, u32[]{:S(2)}, u32[]{:S(2)}) collective-permute-start(f32[168,128]{1,0:T(8,128)S(1)} %constant_dynamic-slice_fusion.11), channel_id=1, source_target_pairs={{0,32},{1,33},{2,34},{3,35},{4,36},{5,37},{6,38},{7,39},{8,40},{9,... | collective-permute-start | bytes 258056 | tf_op jit(solution)/shard_map/ppermute | solution.py:115
  106.0 6.5 %collective-permute-start.12 = (f32[84,128]{1,0:T(8,128)S(1)}, f32[84,128]{1,0:T(8,128)S(1)}, u32[]{:S(2)}, u32[]{:S(2)}) collective-permute-start(f32[84,128]{1,0:T(8,128)S(1)} %constant_dynamic-slice_fusion.17), channel_id=1, source_target_pairs={{0,24},{1,25},{2,26},{3,27},{4,28},{5,29},{6,30},{7,31},{8,16},{9,... | collective-permute-start | bytes 129032 | tf_op jit(solution)/shard_map/ppermute | solution.py:115
  108.1 5.0 %collective-permute-start.24 = (f32[84,128]{1,0:T(8,128)S(1)}, f32[84,128]{1,0:T(8,128)S(1)}, u32[]{:S(2)}, u32[]{:S(2)}) collective-permute-start(f32[84,128]{1,0:T(8,128)S(1)} %constant_dynamic-slice_fusion.10), channel_id=1, source_target_pairs={{0,96},{1,97},{2,98},{3,99},{4,100},{5,101},{6,102},{7,103},{8,104... | collective-permute-start | bytes 129032 | tf_op jit(solution)/shard_map/ppermute | solution.py:115
  114.4 4.4 %collective-permute-start.37 = (f32[42,128]{1,0:T(8,128)S(1)}, f32[42,128]{1,0:T(8,128)S(1)}, u32[]{:S(2)}, u32[]{:S(2)}) collective-permute-start(f32[42,128]{1,0:T(8,128)S(1)} %constant_dynamic-slice_fusion.2), channel_id=1, source_target_pairs={{0,8},{1,9},{2,10},{3,11},{4,12},{5,13},{6,14},{7,15},{8,0},{9,1},... | collective-permute-start | bytes 64520 | tf_op jit(solution)/shard_map/ppermute | solution.py:115
  115.6 4.7 %collective-permute-start.14 = (f32[21,128]{1,0:T(8,128)S(1)}, f32[21,128]{1,0:T(8,128)S(1)}, u32[]{:S(2)}, u32[]{:S(2)}) collective-permute-start(f32[21,128]{1,0:T(8,128)S(1)} %constant_dynamic-slice_fusion.14), channel_id=1, source_target_pairs={{0,96},{1,97},{2,98},{3,99},{4,100},{5,101},{6,102},{7,103},{8,104... | collective-permute-start | bytes 32264 | tf_op jit(solution)/shard_map/ppermute | solution.py:115
  116.6 5.0 %collective-permute-start.26 = (f32[21,128]{1,0:T(8,128)S(1)}, f32[21,128]{1,0:T(8,128)S(1)}, u32[]{:S(2)}, u32[]{:S(2)}) collective-permute-start(f32[21,128]{1,0:T(8,128)S(1)} %constant_dynamic-slice_fusion.7), channel_id=1, source_target_pairs={{0,6},{1,7},{2,4},{3,5},{4,2},{5,3},{6,0},{7,1},{8,14},{9,15},{10,... | collective-permute-start | bytes 32264 | tf_op jit(solution)/shard_map/ppermute | solution.py:115
  121.8 5.0 %collective-permute-start.27 = (bf16[21,128]{1,0:T(8,128)(2,1)S(1)}, bf16[21,128]{1,0:T(8,128)(2,1)S(1)}, u32[]{:S(2)}, u32[]{:S(2)}) collective-permute-start(bf16[21,128]{1,0:T(8,128)(2,1)S(1)} %fusion.28), channel_id=1, source_target_pairs={{0,6},{1,7},{2,4},{3,5},{4,2},{5,3},{6,0},{7,1},{8,14},{9,15},{10,... | collective-permute-start | bytes 16136 | tf_op jit(solution)/shard_map/ppermute | solution.py:123
  127.1 5.2 %collective-permute-start.28 = (bf16[42,128]{1,0:T(8,128)(2,1)S(1)}, bf16[42,128]{1,0:T(8,128)(2,1)S(1)}, u32[]{:S(2)}, u32[]{:S(2)}) collective-permute-start(bf16[42,128]{1,0:T(8,128)(2,1)S(1)} %dynamic_update_slice.127), channel_id=1, source_target_pairs={{0,2},{1,3},{2,0},{3,1},{4,6},{5,7},{6,4},{7,5},{8,10},{9,11},{10,... | collective-permute-start | bytes 32264 | tf_op jit(solution)/shard_map/ppermute | solution.py:123
  127.4 6.6 %collective-permute-start.40 = (bf16[42,128]{1,0:T(8,128)(2,1)S(1)}, bf16[42,128]{1,0:T(8,128)(2,1)S(1)}, u32[]{:S(2)}, u32[]{:S(2)}) collective-permute-start(bf16[42,128]{1,0:T(8,128)(2,1)S(1)} %dynamic_update_slice.139), channel_id=1, source_target_pairs={{0,8},{1,9},{2,10},{3,11},{4,12},{5,13},{6,14},{7,15},{8,0},{9,1},... | collective-permute-start | bytes 32264 | tf_op jit(solution)/shard_map/ppermute | solution.py:123
  128.2 8.1 %collective-permute-start.17 = (bf16[84,128]{1,0:T(8,128)(2,1)S(1)}, bf16[84,128]{1,0:T(8,128)(2,1)S(1)}, u32[]{:S(2)}, u32[]{:S(2)}) collective-permute-start(bf16[84,128]{1,0:T(8,128)(2,1)S(1)} %dynamic_update_slice.117), channel_id=1, source_target_pairs={{0,24},{1,25},{2,26},{3,27},{4,28},{5,29},{6,30},{7,31},{8,16},{9,... | collective-permute-start | bytes 64520 | tf_op jit(solution)/shard_map/ppermute | solution.py:123
  132.5 4.7 %collective-permute-start.29 = (bf16[84,128]{1,0:T(8,128)(2,1)S(1)}, bf16[84,128]{1,0:T(8,128)(2,1)S(1)}, u32[]{:S(2)}, u32[]{:S(2)}) collective-permute-start(bf16[84,128]{1,0:T(8,128)(2,1)S(1)} %dynamic_update_slice.129), channel_id=1, source_target_pairs={{0,96},{1,97},{2,98},{3,99},{4,100},{5,101},{6,102},{7,103},{8,104... | collective-permute-start | bytes 64520 | tf_op jit(solution)/shard_map/ppermute | solution.py:123
  139.6 4.8 %collective-permute-start.19 = (bf16[336,128]{1,0:T(8,128)(2,1)S(1)}, bf16[336,128]{1,0:T(8,128)(2,1)S(1)}, u32[]{:S(2)}, u32[]{:S(2)}) collective-permute-start(bf16[336,128]{1,0:T(8,128)(2,1)S(1)} %constant_dynamic-update-slice_fusion.18), channel_id=1, source_target_pairs={{0,6},{1,7},{2,4},{3,5},{4,2},{5,3},{6,0},{7,1},{8,14},{9,15},{10,... | collective-permute-start | bytes 258056 | tf_op jit(solution)/shard_map/ppermute | solution.py:123
  140.9 4.6 %collective-permute-start.31 = (bf16[336,128]{1,0:T(8,128)(2,1)S(1)}, bf16[336,128]{1,0:T(8,128)(2,1)S(1)}, u32[]{:S(2)}, u32[]{:S(2)}) collective-permute-start(bf16[336,128]{1,0:T(8,128)(2,1)S(1)} %constant_dynamic-update-slice_fusion.12), channel_id=1, source_target_pairs={{0,24},{1,25},{2,26},{3,27},{4,28},{5,29},{6,30},{7,31},{8,16},{9,... | collective-permute-start | bytes 258056 | tf_op jit(solution)/shard_map/ppermute | solution.py:123
  142.6 4.6 %collective-permute-start.43 = (bf16[336,128]{1,0:T(8,128)(2,1)S(1)}, bf16[336,128]{1,0:T(8,128)(2,1)S(1)}, u32[]{:S(2)}, u32[]{:S(2)}) collective-permute-start(bf16[336,128]{1,0:T(8,128)(2,1)S(1)} %constant_dynamic-update-slice_fusion.6), channel_id=1, source_target_pairs={{0,96},{1,97},{2,98},{3,99},{4,100},{5,101},{6,102},{7,103},{8,104... | collective-permute-start | bytes 258056 | tf_op jit(solution)/shard_map/ppermute | solution.py:123
  144.4 4.6 %collective-permute-start.20 = (bf16[672,128]{1,0:T(8,128)(2,1)S(1)}, bf16[672,128]{1,0:T(8,128)(2,1)S(1)}, u32[]{:S(2)}, u32[]{:S(2)}) collective-permute-start(bf16[672,128]{1,0:T(8,128)(2,1)S(1)} %constant_dynamic-update-slice_fusion.16), channel_id=1, source_target_pairs={{0,2},{1,3},{2,0},{3,1},{4,6},{5,7},{6,4},{7,5},{8,10},{9,11},{10,... | collective-permute-start | bytes 516104 | tf_op jit(solution)/shard_map/ppermute | solution.py:123
  147.3 4.3 %collective-permute-start.44 = (bf16[672,128]{1,0:T(8,128)(2,1)S(1)}, bf16[672,128]{1,0:T(8,128)(2,1)S(1)}, u32[]{:S(2)}, u32[]{:S(2)}) collective-permute-start(bf16[672,128]{1,0:T(8,128)(2,1)S(1)} %constant_dynamic-update-slice_fusion.4), channel_id=1, source_target_pairs={{0,32},{1,33},{2,34},{3,35},{4,36},{5,37},{6,38},{7,39},{8,40},{9,... | collective-permute-start | bytes 516104 | tf_op jit(solution)/shard_map/ppermute | solution.py:123
  153.0 25.2 %collective-permute-start.45 = (bf16[4032,128]{1,0:T(8,128)(2,1)}, bf16[4032,128]{1,0:T(8,128)(2,1)}, u32[]{:S(2)}, u32[]{:S(2)}) collective-permute-start(bf16[4032,128]{1,0:T(8,128)(2,1)} %get-tuple-element.12), channel_id=1, source_target_pairs={{0,1},{1,0},{2,3},{3,2},{4,5},{5,4},{6,7},{7,6},{8,9},{9,8},{10,11... | collective-permute-start | bytes 3096584 | tf_op jit(solution)/shard_map/ppermute | solution.py:126
  (43 other events, 227.5 us)

commit v3 on v2

--- a/solution.py
+++ b/solution.py
@@ -22,14 +22,23 @@
     return g.reshape(4, PX * PY * PZ, channels)
 
 
-def padded(grid):
+def padded_many(*grids):
     count = lax.axis_size("range")
     forward = [(i, i + 1) for i in range(count - 1)]
     backward = [(i + 1, i) for i in range(count - 1)]
-    low = lax.ppermute(grid[:, :, PZ - 1 :], "range", forward)
-    high = lax.ppermute(grid[:, :, :1], "range", backward)
-    wide = jnp.concatenate([low, grid, high], axis=2)
-    return jnp.pad(wide, ((1, 1), (1, 1), (0, 0), (0, 0)))
+    low = lax.ppermute(jnp.concatenate([g[:, :, PZ - 1 :] for g in grids], -1), "range", forward)
+    high = lax.ppermute(jnp.concatenate([g[:, :, :1] for g in grids], -1), "range", backward)
+    out = []
+    for n, grid in enumerate(grids):
+        width = grid.shape[-1]
+        piece = slice(n * width, (n + 1) * width)
+        wide = jnp.concatenate([low[..., piece], grid, high[..., piece]], axis=2)
+        out.append(jnp.pad(wide, ((1, 1), (1, 1), (0, 0), (0, 0))))
+    return out
+
+
+def padded(grid):
+    return padded_many(grid)[0]
 
 
 def z_columns(pad):
@@ -61,7 +70,7 @@
     return jnp.concatenate(terms, 0)
 
 AXIS_SHIFT = {"y": 1, "x": 3, "z": 5}
-PART_ORDERS = (("y", "x", "z"), ("x", "z", "y"), ("z", "y", "x"))
+PART_ORDERS = (("y", "x", "z"),)
 
 
 def coordinate(index, shift):
@@ -150,7 +159,9 @@
     hidden = jnp.dot(patches, down_flat, preferred_element_type=f32).astype(bf16)
     hidden_grid = hidden.reshape(2 * PX, 2 * PY, PZ, channels)
 
-    hidden_cols = z_columns(padded(hidden_grid))
+    cot_grid = to_grid(cotangent[block_at])
+    hidden_pad, cot_pad = padded_many(hidden_grid, cot_grid)
+    hidden_cols = z_columns(hidden_pad)
     pre_act = conv_apply(hidden_cols, first_w)
     activated = jax.nn.silu(pre_act).astype(bf16)
     act_cols = z_columns(padded(activated.reshape(2 * PX, 2 * PY, PZ, channels)))
@@ -158,9 +169,8 @@
         hidden.astype(f32) + conv_apply(act_cols, second_w)
     ).astype(bf16)
 
-    cot_grid = to_grid(cotangent[block_at])
     cot_rows = cot_grid.reshape(-1, channels)
-    cot_cols = z_columns(padded(cot_grid))
+    cot_cols = z_columns(cot_pad)
     back_act = conv_apply(cot_cols, reversed_kernel(second_w))
     sigmoid_pre = jax.nn.sigmoid(pre_act)
     d_pre = (back_act * sigmoid_pre * (1.0 + pre_act * (1.0 - sigmoid_pre))).astype(bf16)
@@ -190,7 +200,7 @@
     )
     limit = jnp.float32(channels * math.sqrt(62.0))
     total_values = raw_grads.size
-    rows = 8064
+    rows = total_values // channels
     flat = jnp.pad(raw_grads.reshape(-1), (0, rows * channels - total_values)).reshape(rows, channels)
     summed = torus_psum(flat).reshape(-1)[:total_values].reshape(raw_grads.shape)
     grad_total = jnp.sqrt(jnp.sum(summed * summed))

time: 186 us -> 197 us (1.059)
  waiting for transfers between devices: 15.2 us -> 68 us
  starting transfers between devices: 96.1 us -> 61.6 us
  matrix products: 27 us -> 19 us
  other arithmetic: 8.27 us -> 11 us
    ppermute x18 -> x6, waiting for transfers between devices: 4.97 us -> 43.9 us  [torus_psum(): part = keep + lax.ppermute(send, 'range', perm)]
    ppermute x18 -> x6, starting transfers between devices: 45.1 us -> 24.3 us  [torus_psum(): part = keep + lax.ppermute(send, 'range', perm)]
    ppermute x18 -> x6, waiting for transfers between devices: 7.01 us -> 17.7 us  [torus_psum(): part = join_halves(part, lax.ppermute(part, 'range', perm), bit)]
    ppermute x18 -> x6, starting transfers between devices: 16 us -> 7.5 us  [torus_psum(): part = join_halves(part, lax.ppermute(part, 'range', perm), bit)]
    dot_general x36, matrix products: 19.1 us -> 12 us  [conv_apply(): jnp.dot(xy_window(zcols, sx, sy), taps[sx, sy], preferred_element_type=jn...]
    ppermute x8 -> x6, starting transfers between devices: 23.4 us -> 17.8 us  [the longest x3 11.9 us: padded_many(): lax.ppermute(jnp.concatenate([g[:, :, PZ - 1:] for g in grids], -1), 'ran...]
    add x15 -> x5, other arithmetic: 0.29 us -> 4.19 us  [torus_psum(): part = keep + lax.ppermute(send, 'range', perm)]
    ppermute x1, waiting for transfers between devices: 0.98 us -> 4.19 us  [torus_psum(): y = keep + lax.ppermute(send, 'range', core_perm)]
  transfers between devices with their start and end apart: 46 -> 20, of which waited for: 13 -> 14; matrix products, arithmetic and copies ran while one was open for 21% -> 11% of each run, Pallas kernels for 0% -> 0%
where the time goes in v3:
time: 197 us; the launch traced here: 196 us
  waiting for transfers between devices  68 us (35%)
  starting transfers between devices  61.6 us (31%)
  local copies, waits for them, and re-layouts  34.1 us (17%)
  matrix products  19 us (10%)
  other arithmetic  11 us (6%)
  between operations  2.73 us (1%)
    ppermute x6, waiting for transfers between devices, torus_psum(): part = keep + lax.ppermute(send, 'range', perm)  43.9 us
    ppermute x6, starting transfers between devices, torus_psum(): part = keep + lax.ppermute(send, 'range', perm)  24.3 us
    ppermute x6, waiting for transfers between devices, torus_psum(): part = join_halves(part, lax.ppermute(part, 'range', perm), bit)  17.7 us
    dot_general x36, matrix products, conv_apply(): jnp.dot(xy_window(zcols, sx, sy), taps[sx, sy], preferred_element_type=jn...  12 us
    ppermute x1, starting transfers between devices, torus_psum(): lax.ppermute(y, 'range', core_perm)  12 us
    ppermute x3, starting transfers between devices, padded_many(): lax.ppermute(jnp.concatenate([g[:, :, PZ - 1:] for g in grids], -1), 'ran...  11.9 us
    ppermute x6, starting transfers between devices, torus_psum(): part = join_halves(part, lax.ppermute(part, 'range', perm), bit)  7.5 us
    unnamed x68, local copies, waits for them, and re-layouts  6.57 us
  transfers between devices with their start and end apart: 20, of which 14 were waited for; matrix products, arithmetic and copies ran while one was open for 11% of the time, Pallas kernels for 0%

profile of v3, /device:TPU:1, one launch (start us, length us, event | category | flops | bytes accessed | tf_op | source)
XLA Modules:
  0.0 196.4 jit_solution(6487908699243628755)
XLA Ops:
  8.0 4.6 %collective-permute-start = (bf16[8,8,1,256]{3,2,1,0:T(2,128)(2,1)S(1)}, bf16[8,8,1,256]{3,2,1,0:T(2,128)(2,1)S(1)}, u32[]{:S(2)}, u32[]{:S(2)}) collective-permute-start(bf16[8,8,1,256]{3,2,1,0:T(2,128)(2,1)S(1)} %pad_maximum_fusion.5), channel_id=1, source_target_pairs={{0,1},{1,2},{2,3},{3,4},{4,5},{5,6},{6,7},{7,8},{8,9},{9,10},{10,1... | collective-permute-start | bytes 98312 | tf_op jit(solution)/shard_map/ppermute | solution.py:29
  12.6 1.9 collective-permute-start.1
  31.0 3.6 %collective-permute-start.2 = (bf16[8,8,1,128]{3,2,1,0:T(2,128)(2,1)S(1)}, bf16[8,8,1,128]{3,2,1,0:T(2,128)(2,1)S(1)}, u32[]{:S(2)}, u32[]{:S(2)}) collective-permute-start(bf16[8,8,1,128]{3,2,1,0:T(2,128)(2,1)S(1)} %get-tuple-element.59), channel_id=1, source_target_pairs={{0,1},{1,2},{2,3},{3,4},{4,5},{5,6},{6,7},{7,8},{8,9},{9,10},{10,1... | collective-permute-start | bytes 49160 | tf_op jit(solution)/shard_map/ppermute | solution.py:29
  34.7 1.9 collective-permute-start.3
  36.7 3.6 %collective-permute-start.4 = (bf16[8,8,1,128]{3,2,1,0:T(2,128)(2,1)S(1)}, bf16[8,8,1,128]{3,2,1,0:T(2,128)(2,1)S(1)}, u32[]{:S(2)}, u32[]{:S(2)}) collective-permute-start(bf16[8,8,1,128]{3,2,1,0:T(2,128)(2,1)S(1)} %get-tuple-element.57), channel_id=1, source_target_pairs={{0,1},{1,2},{2,3},{3,4},{4,5},{5,6},{6,7},{7,8},{8,9},{9,10},{10,1... | collective-permute-start | bytes 49160 | tf_op jit(solution)/shard_map/ppermute | solution.py:29
  40.3 2.1 %collective-permute-start.5 = (bf16[8,8,1,128]{3,2,1,0:T(2,128)(2,1)S(1)}, bf16[8,8,1,128]{3,2,1,0:T(2,128)(2,1)S(1)}, u32[]{:S(2)}, u32[]{:S(2)}) collective-permute-start(bf16[8,8,1,128]{3,2,1,0:T(2,128)(2,1)S(1)} %get-tuple-element.58), channel_id=1, source_target_pairs={{1,0},{2,1},{3,2},{4,3},{5,4},{6,5},{7,6},{8,7},{9,8},{10,9},{11,1... | collective-permute-start | bytes 49160 | tf_op jit(solution)/shard_map/ppermute | solution.py:30
  43.3 2.2 %collective-permute-done.5 = bf16[8,8,1,128]{3,2,1,0:T(2,128)(2,1)S(1)} collective-permute-done((bf16[8,8,1,128]{3,2,1,0:T(2,128)(2,1)S(1)}, bf16[8,8,1,128]{3,2,1,0:T(2,128)(2,1)S(1)}, u32[]{:S(2)}, u32[]{:S(2)}) %collective-permute-start.5) | collective-permute-done | bytes 16416 | tf_op jit(solution)/shard_map/ppermute | solution.py:30
  53.1 1.8 copy-done.2
  54.9 4.2 %collective-permute-done.6 = f32[3968,128]{1,0:T(8,128)} collective-permute-done((f32[3968,128]{1,0:T(8,128)S(1)}, f32[3968,128]{1,0:T(8,128)}, u32[]{:S(2)}, u32[]{:S(2)}) %collective-permute-start.6) | collective-permute-done | bytes 2031648 | tf_op jit(solution)/shard_map/ppermute | solution.py:116
  59.1 2.4 %dynamic-slice_add_fusion = f32[3968,128]{1,0:T(8,128)S(1)} fusion(f32[3968,128]{1,0:T(8,128)} %collective-permute-done.6, f32[7936,128]{1,0:T(8,128)} %bitcast.285, s32[]{:T(128)S(6)} %select_n.82), kind=kLoop, calls=%fused_computation.10 | loop fusion | flops 507904 | bytes 6094852 | tf_op jit(solution)/shard_map/add | solution.py:116
  62.9 22.7 %collective-permute-done.7 = f32[1984,128]{1,0:T(8,128)} collective-permute-done((f32[1984,128]{1,0:T(8,128)S(1)}, f32[1984,128]{1,0:T(8,128)}, u32[]{:S(2)}, u32[]{:S(2)}) %collective-permute-start.7) | collective-permute-done | bytes 1015840 | tf_op jit(solution)/shard_map/ppermute | solution.py:124
  87.8 8.6 %collective-permute-start.8 = (f32[992,128]{1,0:T(8,128)}, f32[992,128]{1,0:T(8,128)}, u32[]{:S(2)}, u32[]{:S(2)}) collective-permute-start(f32[992,128]{1,0:T(8,128)} %constant_dynamic-slice_fusion.4), channel_id=1, source_target_pairs={{0,6},{1,7},{2,4},{3,5},{4,2},{5,3},{6,0},{7,1},{8,14},{9,15},{10,... | collective-permute-start | bytes 1523720 | tf_op jit(solution)/shard_map/ppermute | solution.py:124
  96.4 11.3 %collective-permute-done.8 = f32[992,128]{1,0:T(8,128)} collective-permute-done((f32[992,128]{1,0:T(8,128)}, f32[992,128]{1,0:T(8,128)}, u32[]{:S(2)}, u32[]{:S(2)}) %collective-permute-start.8) | collective-permute-done | bytes 507936 | tf_op jit(solution)/shard_map/ppermute | solution.py:124
  107.7 1.9 dynamic-slice_add_fusion.2
  112.5 4.2 %collective-permute-done.9 = f32[496,128]{1,0:T(8,128)S(1)} collective-permute-done((f32[496,128]{1,0:T(8,128)S(1)}, f32[496,128]{1,0:T(8,128)S(1)}, u32[]{:S(2)}, u32[]{:S(2)}) %collective-permute-start.9) | collective-permute-done | bytes 253984 | tf_op jit(solution)/shard_map/ppermute | solution.py:124
  117.8 9.2 %collective-permute-start.10 = (f32[248,128]{1,0:T(8,128)S(1)}, f32[248,128]{1,0:T(8,128)S(1)}, u32[]{:S(2)}, u32[]{:S(2)}) collective-permute-start(f32[248,128]{1,0:T(8,128)S(1)} %constant_dynamic-slice_fusion.2), channel_id=1, source_target_pairs={{0,24},{1,25},{2,26},{3,27},{4,28},{5,29},{6,30},{7,31},{8,16},{9,... | collective-permute-start | bytes 380936 | tf_op jit(solution)/shard_map/ppermute | solution.py:124
  127.0 2.3 %collective-permute-done.10 = f32[248,128]{1,0:T(8,128)S(1)} collective-permute-done((f32[248,128]{1,0:T(8,128)S(1)}, f32[248,128]{1,0:T(8,128)S(1)}, u32[]{:S(2)}, u32[]{:S(2)}) %collective-permute-start.10) | collective-permute-done | bytes 127008 | tf_op jit(solution)/shard_map/ppermute | solution.py:124
  129.4 1.7 collective-permute-start.11
  131.1 1.6 collective-permute-done.11
  132.8 2.0 %collective-permute-start.12 = (f32[62,128]{1,0:T(8,128)S(1)}, f32[62,128]{1,0:T(8,128)S(1)}, u32[]{:S(2)}, u32[]{:S(2)}) collective-permute-start(f32[62,128]{1,0:T(8,128)S(1)} %constant_dynamic-slice_fusion), channel_id=1, source_target_pairs={{0,96},{1,97},{2,98},{3,99},{4,100},{5,101},{6,102},{7,103},{8,104... | collective-permute-start | bytes 95240 | tf_op jit(solution)/shard_map/ppermute | solution.py:124
  135.1 1.7 collective-permute-done.12
  136.8 2.0 %collective-permute-start.13 = (bf16[62,128]{1,0:T(8,128)(2,1)S(1)}, bf16[62,128]{1,0:T(8,128)(2,1)S(1)}, u32[]{:S(2)}, u32[]{:S(2)}) collective-permute-start(bf16[62,128]{1,0:T(8,128)(2,1)S(1)} %add_convert_fusion), channel_id=1, source_target_pairs={{0,96},{1,97},{2,98},{3,99},{4,100},{5,101},{6,102},{7,103},{8,104... | collective-permute-start | bytes 47624 | tf_op jit(solution)/shard_map/ppermute | solution.py:132
  141.6 2.1 %collective-permute-done.14 = bf16[124,128]{1,0:T(8,128)(2,1)S(1)} collective-permute-done((bf16[124,128]{1,0:T(8,128)(2,1)S(1)}, bf16[124,128]{1,0:T(8,128)(2,1)S(1)}, u32[]{:S(2)}, u32[]{:S(2)}) %collective-permute-start.14) | collective-permute-done | bytes 31776 | tf_op jit(solution)/shard_map/ppermute | solution.py:132
  143.9 2.8 %collective-permute-start.15 = (bf16[248,128]{1,0:T(8,128)(2,1)S(1)}, bf16[248,128]{1,0:T(8,128)(2,1)S(1)}, u32[]{:S(2)}, u32[]{:S(2)}) collective-permute-start(bf16[248,128]{1,0:T(8,128)(2,1)S(1)} %dynamic_update_slice.45), channel_id=1, source_target_pairs={{0,24},{1,25},{2,26},{3,27},{4,28},{5,29},{6,30},{7,31},{8,16},{9,... | collective-permute-start | bytes 190472 | tf_op jit(solution)/shard_map/ppermute | solution.py:132
  148.7 3.4 %collective-permute-done.16 = bf16[496,128]{1,0:T(8,128)(2,1)S(1)} collective-permute-done((bf16[496,128]{1,0:T(8,128)(2,1)S(1)}, bf16[496,128]{1,0:T(8,128)(2,1)S(1)}, u32[]{:S(2)}, u32[]{:S(2)}) %collective-permute-start.16) | collective-permute-done | bytes 127008 | tf_op jit(solution)/shard_map/ppermute | solution.py:132
  152.2 2.2 %collective-permute-start.17 = (bf16[992,128]{1,0:T(8,128)(2,1)S(1)}, bf16[992,128]{1,0:T(8,128)(2,1)S(1)}, u32[]{:S(2)}, u32[]{:S(2)}) collective-permute-start(bf16[992,128]{1,0:T(8,128)(2,1)S(1)} %constant_dynamic-update-slice_fusion.6), channel_id=1, source_target_pairs={{0,6},{1,7},{2,4},{3,5},{4,2},{5,3},{6,0},{7,1},{8,14},{9,15},{10,... | collective-permute-start | bytes 761864 | tf_op jit(solution)/shard_map/ppermute | solution.py:132
  154.8 3.8 %collective-permute-done.17 = bf16[992,128]{1,0:T(8,128)(2,1)S(1)} collective-permute-done((bf16[992,128]{1,0:T(8,128)(2,1)S(1)}, bf16[992,128]{1,0:T(8,128)(2,1)S(1)}, u32[]{:S(2)}, u32[]{:S(2)}) %collective-permute-start.17) | collective-permute-done | bytes 253984 | tf_op jit(solution)/shard_map/ppermute | solution.py:132
  161.6 5.5 %collective-permute-done.18 = bf16[1984,128]{1,0:T(8,128)(2,1)S(1)} collective-permute-done((bf16[1984,128]{1,0:T(8,128)(2,1)S(1)}, bf16[1984,128]{1,0:T(8,128)(2,1)S(1)}, u32[]{:S(2)}, u32[]{:S(2)}) %collective-permute-start.18) | collective-permute-done | bytes 507936 | tf_op jit(solution)/shard_map/ppermute | solution.py:132
  167.9 12.0 %collective-permute-start.19 = (bf16[3968,128]{1,0:T(8,128)(2,1)}, bf16[3968,128]{1,0:T(8,128)(2,1)}, u32[]{:S(2)}, u32[]{:S(2)}) collective-permute-start(bf16[3968,128]{1,0:T(8,128)(2,1)} %constant_dynamic-update-slice_fusion.2), channel_id=1, source_target_pairs={{0,1},{1,0},{2,3},{3,2},{4,5},{5,4},{6,7},{7,6},{8,9},{9,8},{10,11... | collective-permute-start | bytes 3047432 | tf_op jit(solution)/shard_map/ppermute | solution.py:135
  185.1 1.7 gather_fusion.4
  191.0 1.6 fusion
  193.6 2.0 %fusion.32 = (f32[3456,128]{1,0:T(8,128)}, f32[3456,128]{1,0:T(8,128)}) fusion(f32[7936,128]{1,0:T(8,128)S(1)} %convert_multiply_fusion), kind=kLoop, calls=%fused_computation.184 | loop fusion | bytes 7077888 | tf_op jit(solution)/shard_map/slice | solution.py:209
  (224 shorter events, 58.8 us)
Async XLA Ops:
  5.8 8.8 %copy-start.19 = (bf16[27,128,128]{2,1,0:T(8,128)(2,1)S(1)}, bf16[27,128,128]{2,1,0:T(8,128)(2,1)}, u32[]{:S(2)}) copy-start(bf16[27,128,128]{2,1,0:T(8,128)(2,1)} %param.13) | copy-start | bytes 2654212
  6.3 14.9 %copy-start.25 = (bf16[512,128]{1,0:T(8,128)(2,1)}, bf16[512,128]{1,0:T(8,128)(2,1)S(1)}, u32[]{:S(2)}) copy-start(bf16[512,128]{1,0:T(8,128)(2,1)S(1)} %convolution_convert_fusion.1) | copy-start | bytes 393220
  8.0 12.3 %collective-permute-start = (bf16[8,8,1,256]{3,2,1,0:T(2,128)(2,1)S(1)}, bf16[8,8,1,256]{3,2,1,0:T(2,128)(2,1)S(1)}, u32[]{:S(2)}, u32[]{:S(2)}) collective-permute-start(bf16[8,8,1,256]{3,2,1,0:T(2,128)(2,1)S(1)} %pad_maximum_fusion.5), channel_id=1, source_target_pairs={{0,1},{1,2},{2,3},{3,4},{4,5},{5,6},{6,7},{7,8},{8,9},{9,10},{10,1... | collective-permute-start | bytes 98312 | tf_op jit(solution)/shard_map/ppermute | solution.py:29
  12.6 7.7 %collective-permute-start.1 = (bf16[8,8,1,256]{3,2,1,0:T(2,128)(2,1)S(1)}, bf16[8,8,1,256]{3,2,1,0:T(2,128)(2,1)S(1)}, u32[]{:S(2)}, u32[]{:S(2)}) collective-permute-start(bf16[8,8,1,256]{3,2,1,0:T(2,128)(2,1)S(1)} %pad_maximum_fusion.6), channel_id=1, source_target_pairs={{1,0},{2,1},{3,2},{4,3},{5,4},{6,5},{7,6},{8,7},{9,8},{10,9},{11,1... | collective-permute-start | bytes 98312 | tf_op jit(solution)/shard_map/ppermute | solution.py:30
  31.0 11.4 %collective-permute-start.2 = (bf16[8,8,1,128]{3,2,1,0:T(2,128)(2,1)S(1)}, bf16[8,8,1,128]{3,2,1,0:T(2,128)(2,1)S(1)}, u32[]{:S(2)}, u32[]{:S(2)}) collective-permute-start(bf16[8,8,1,128]{3,2,1,0:T(2,128)(2,1)S(1)} %get-tuple-element.59), channel_id=1, source_target_pairs={{0,1},{1,2},{2,3},{3,4},{4,5},{5,6},{6,7},{7,8},{8,9},{9,10},{10,1... | collective-permute-start | bytes 49160 | tf_op jit(solution)/shard_map/ppermute | solution.py:29
  34.7 7.8 %collective-permute-start.3 = (bf16[8,8,1,128]{3,2,1,0:T(2,128)(2,1)S(1)}, bf16[8,8,1,128]{3,2,1,0:T(2,128)(2,1)S(1)}, u32[]{:S(2)}, u32[]{:S(2)}) collective-permute-start(bf16[8,8,1,128]{3,2,1,0:T(2,128)(2,1)S(1)} %get-tuple-element.60), channel_id=1, source_target_pairs={{1,0},{2,1},{3,2},{4,3},{5,4},{6,5},{7,6},{8,7},{9,8},{10,9},{11,1... | collective-permute-start | bytes 49160 | tf_op jit(solution)/shard_map/ppermute | solution.py:30
  36.7 6.6 %collective-permute-start.4 = (bf16[8,8,1,128]{3,2,1,0:T(2,128)(2,1)S(1)}, bf16[8,8,1,128]{3,2,1,0:T(2,128)(2,1)S(1)}, u32[]{:S(2)}, u32[]{:S(2)}) collective-permute-start(bf16[8,8,1,128]{3,2,1,0:T(2,128)(2,1)S(1)} %get-tuple-element.57), channel_id=1, source_target_pairs={{0,1},{1,2},{2,3},{3,4},{4,5},{5,6},{6,7},{7,8},{8,9},{9,10},{10,1... | collective-permute-start | bytes 49160 | tf_op jit(solution)/shard_map/ppermute | solution.py:29
  40.3 5.2 %collective-permute-start.5 = (bf16[8,8,1,128]{3,2,1,0:T(2,128)(2,1)S(1)}, bf16[8,8,1,128]{3,2,1,0:T(2,128)(2,1)S(1)}, u32[]{:S(2)}, u32[]{:S(2)}) collective-permute-start(bf16[8,8,1,128]{3,2,1,0:T(2,128)(2,1)S(1)} %get-tuple-element.58), channel_id=1, source_target_pairs={{1,0},{2,1},{3,2},{4,3},{5,4},{6,5},{7,6},{8,7},{9,8},{10,9},{11,1... | collective-permute-start | bytes 49160 | tf_op jit(solution)/shard_map/ppermute | solution.py:30
  54.9 4.2 %collective-permute-start.6 = (f32[3968,128]{1,0:T(8,128)S(1)}, f32[3968,128]{1,0:T(8,128)}, u32[]{:S(2)}, u32[]{:S(2)}) collective-permute-start(f32[3968,128]{1,0:T(8,128)S(1)} %constant_dynamic-slice_fusion.6), channel_id=1, source_target_pairs={{0,1},{1,0},{2,3},{3,2},{4,5},{5,4},{6,7},{7,6},{8,9},{9,8},{10,11... | collective-permute-start | bytes 6094856 | tf_op jit(solution)/shard_map/ppermute | solution.py:116
  61.6 24.1 %collective-permute-start.7 = (f32[1984,128]{1,0:T(8,128)S(1)}, f32[1984,128]{1,0:T(8,128)}, u32[]{:S(2)}, u32[]{:S(2)}) collective-permute-start(f32[1984,128]{1,0:T(8,128)S(1)} %constant_dynamic-slice_fusion.5), channel_id=1, source_target_pairs={{0,2},{1,3},{2,0},{3,1},{4,6},{5,7},{6,4},{7,5},{8,10},{9,11},{10,... | collective-permute-start | bytes 3047432 | tf_op jit(solution)/shard_map/ppermute | solution.py:124
  87.8 19.9 %collective-permute-start.8 = (f32[992,128]{1,0:T(8,128)}, f32[992,128]{1,0:T(8,128)}, u32[]{:S(2)}, u32[]{:S(2)}) collective-permute-start(f32[992,128]{1,0:T(8,128)} %constant_dynamic-slice_fusion.4), channel_id=1, source_target_pairs={{0,6},{1,7},{2,4},{3,5},{4,2},{5,3},{6,0},{7,1},{8,14},{9,15},{10,... | collective-permute-start | bytes 1523720 | tf_op jit(solution)/shard_map/ppermute | solution.py:124
  96.4 38.4 %copy-start.18 = (bf16[8,8,8,384]{3,2,1,0:T(8,128)(2,1)S(1)}, bf16[8,8,8,384]{3,2,1,0:T(8,128)(2,1)}, u32[]{:S(2)}) copy-start(bf16[8,8,8,384]{3,2,1,0:T(8,128)(2,1)} %copy-done.17) | copy-start | bytes 1179652
  96.4 38.4 %copy-start.20 = (bf16[27,128,128]{2,1,0:T(8,128)(2,1)S(1)}, bf16[27,128,128]{2,1,0:T(8,128)(2,1)}, u32[]{:S(2)}) copy-start(bf16[27,128,128]{2,1,0:T(8,128)(2,1)} %param.13) | copy-start | bytes 2654212
  109.5 29.3 %copy-start.16 = (bf16[8,8,8,384]{3,2,1,0:T(8,128)(2,1)S(1)}, bf16[8,8,8,384]{3,2,1,0:T(8,128)(2,1)}, u32[]{:S(2)}) copy-start(bf16[8,8,8,384]{3,2,1,0:T(8,128)(2,1)} %copy-done.15) | copy-start | bytes 1179652
  110.6 6.2 %collective-permute-start.9 = (f32[496,128]{1,0:T(8,128)S(1)}, f32[496,128]{1,0:T(8,128)S(1)}, u32[]{:S(2)}, u32[]{:S(2)}) collective-permute-start(f32[496,128]{1,0:T(8,128)S(1)} %constant_dynamic-slice_fusion.3), channel_id=1, source_target_pairs={{0,8},{1,9},{2,10},{3,11},{4,12},{5,13},{6,14},{7,15},{8,0},{9,1},... | collective-permute-start | bytes 761864 | tf_op jit(solution)/shard_map/ppermute | solution.py:124
  112.5 28.4 %copy-start.14 = (bf16[8,8,8,384]{3,2,1,0:T(8,128)(2,1)S(1)}, bf16[8,8,8,384]{3,2,1,0:T(8,128)(2,1)}, u32[]{:S(2)}) copy-start(bf16[8,8,8,384]{3,2,1,0:T(8,128)(2,1)} %copy-done.13) | copy-start | bytes 1179652
  117.8 11.6 %collective-permute-start.10 = (f32[248,128]{1,0:T(8,128)S(1)}, f32[248,128]{1,0:T(8,128)S(1)}, u32[]{:S(2)}, u32[]{:S(2)}) collective-permute-start(f32[248,128]{1,0:T(8,128)S(1)} %constant_dynamic-slice_fusion.2), channel_id=1, source_target_pairs={{0,24},{1,25},{2,26},{3,27},{4,28},{5,29},{6,30},{7,31},{8,16},{9,... | collective-permute-start | bytes 380936 | tf_op jit(solution)/shard_map/ppermute | solution.py:124
  129.4 3.4 %collective-permute-start.11 = (f32[124,128]{1,0:T(8,128)S(1)}, f32[124,128]{1,0:T(8,128)S(1)}, u32[]{:S(2)}, u32[]{:S(2)}) collective-permute-start(f32[124,128]{1,0:T(8,128)S(1)} %constant_dynamic-slice_fusion.1), channel_id=1, source_target_pairs={{0,32},{1,33},{2,34},{3,35},{4,36},{5,37},{6,38},{7,39},{8,40},{9,... | collective-permute-start | bytes 190472 | tf_op jit(solution)/shard_map/ppermute | solution.py:124
  132.8 4.1 %collective-permute-start.12 = (f32[62,128]{1,0:T(8,128)S(1)}, f32[62,128]{1,0:T(8,128)S(1)}, u32[]{:S(2)}, u32[]{:S(2)}) collective-permute-start(f32[62,128]{1,0:T(8,128)S(1)} %constant_dynamic-slice_fusion), channel_id=1, source_target_pairs={{0,96},{1,97},{2,98},{3,99},{4,100},{5,101},{6,102},{7,103},{8,104... | collective-permute-start | bytes 95240 | tf_op jit(solution)/shard_map/ppermute | solution.py:124
  134.8 13.5 %copy-start.12 = (bf16[8,8,8,384]{3,2,1,0:T(8,128)(2,1)S(1)}, bf16[8,8,8,384]{3,2,1,0:T(8,128)(2,1)}, u32[]{:S(2)}) copy-start(bf16[8,8,8,384]{3,2,1,0:T(8,128)(2,1)} %copy-done.11) | copy-start | bytes 1179652
  136.8 3.9 %collective-permute-start.13 = (bf16[62,128]{1,0:T(8,128)(2,1)S(1)}, bf16[62,128]{1,0:T(8,128)(2,1)S(1)}, u32[]{:S(2)}, u32[]{:S(2)}) collective-permute-start(bf16[62,128]{1,0:T(8,128)(2,1)S(1)} %add_convert_fusion), channel_id=1, source_target_pairs={{0,96},{1,97},{2,98},{3,99},{4,100},{5,101},{6,102},{7,103},{8,104... | collective-permute-start | bytes 47624 | tf_op jit(solution)/shard_map/ppermute | solution.py:132
  139.1 15.3 %copy-start.10 = (bf16[8,8,8,384]{3,2,1,0:T(8,128)(2,1)S(1)}, bf16[8,8,8,384]{3,2,1,0:T(8,128)(2,1)}, u32[]{:S(2)}) copy-start(bf16[8,8,8,384]{3,2,1,0:T(8,128)(2,1)} %copy-done.9) | copy-start | bytes 1179652
  140.8 2.8 %collective-permute-start.14 = (bf16[124,128]{1,0:T(8,128)(2,1)S(1)}, bf16[124,128]{1,0:T(8,128)(2,1)S(1)}, u32[]{:S(2)}, u32[]{:S(2)}) collective-permute-start(bf16[124,128]{1,0:T(8,128)(2,1)S(1)} %dynamic_update_slice.43), channel_id=1, source_target_pairs={{0,32},{1,33},{2,34},{3,35},{4,36},{5,37},{6,38},{7,39},{8,40},{9,... | collective-permute-start | bytes 95240 | tf_op jit(solution)/shard_map/ppermute | solution.py:132
  143.9 4.4 %collective-permute-start.15 = (bf16[248,128]{1,0:T(8,128)(2,1)S(1)}, bf16[248,128]{1,0:T(8,128)(2,1)S(1)}, u32[]{:S(2)}, u32[]{:S(2)}) collective-permute-start(bf16[248,128]{1,0:T(8,128)(2,1)S(1)} %dynamic_update_slice.45), channel_id=1, source_target_pairs={{0,24},{1,25},{2,26},{3,27},{4,28},{5,29},{6,30},{7,31},{8,16},{9,... | collective-permute-start | bytes 190472 | tf_op jit(solution)/shard_map/ppermute | solution.py:132
  148.3 3.9 %collective-permute-start.16 = (bf16[496,128]{1,0:T(8,128)(2,1)S(1)}, bf16[496,128]{1,0:T(8,128)(2,1)S(1)}, u32[]{:S(2)}, u32[]{:S(2)}) collective-permute-start(bf16[496,128]{1,0:T(8,128)(2,1)S(1)} %constant_dynamic-update-slice_fusion.8), channel_id=1, source_target_pairs={{0,8},{1,9},{2,10},{3,11},{4,12},{5,13},{6,14},{7,15},{8,0},{9,1},... | collective-permute-start | bytes 380936 | tf_op jit(solution)/shard_map/ppermute | solution.py:132
  148.6 10.3 %copy-start.8 = (bf16[8,8,8,384]{3,2,1,0:T(8,128)(2,1)S(1)}, bf16[8,8,8,384]{3,2,1,0:T(8,128)(2,1)}, u32[]{:S(2)}) copy-start(bf16[8,8,8,384]{3,2,1,0:T(8,128)(2,1)} %copy-done.7) | copy-start | bytes 1179652
  152.1 7.1 %copy-start.28 = (bf16[512,128]{1,0:T(8,128)(2,1)S(1)}, bf16[512,128]{1,0:T(8,128)(2,1)}, u32[]{:S(2)}) copy-start(bf16[512,128]{1,0:T(8,128)(2,1)} %copy-done.27) | copy-start | bytes 393220
  152.1 7.1 %copy-start.30 = (bf16[8,128,128]{2,1,0:T(8,128)(2,1)S(1)}, bf16[8,128,128]{2,1,0:T(8,128)(2,1)}, u32[]{:S(2)}) copy-start(bf16[8,128,128]{2,1,0:T(8,128)(2,1)} %param.11) | copy-start | bytes 786436
  152.2 6.4 %collective-permute-start.17 = (bf16[992,128]{1,0:T(8,128)(2,1)S(1)}, bf16[992,128]{1,0:T(8,128)(2,1)S(1)}, u32[]{:S(2)}, u32[]{:S(2)}) collective-permute-start(bf16[992,128]{1,0:T(8,128)(2,1)S(1)} %constant_dynamic-update-slice_fusion.6), channel_id=1, source_target_pairs={{0,6},{1,7},{2,4},{3,5},{4,2},{5,3},{6,0},{7,1},{8,14},{9,15},{10,... | collective-permute-start | bytes 761864 | tf_op jit(solution)/shard_map/ppermute | solution.py:132
  158.6 8.5 %collective-permute-start.18 = (bf16[1984,128]{1,0:T(8,128)(2,1)S(1)}, bf16[1984,128]{1,0:T(8,128)(2,1)S(1)}, u32[]{:S(2)}, u32[]{:S(2)}) collective-permute-start(bf16[1984,128]{1,0:T(8,128)(2,1)S(1)} %constant_dynamic-update-slice_fusion.4), channel_id=1, source_target_pairs={{0,2},{1,3},{2,0},{3,1},{4,6},{5,7},{6,4},{7,5},{8,10},{9,11},{10,... | collective-permute-start | bytes 1523720 | tf_op jit(solution)/shard_map/ppermute | solution.py:132
  159.7 20.2 %copy-start.6 = (bf16[8,8,8,384]{3,2,1,0:T(8,128)(2,1)S(1)}, bf16[8,8,8,384]{3,2,1,0:T(8,128)(2,1)}, u32[]{:S(2)}) copy-start(bf16[8,8,8,384]{3,2,1,0:T(8,128)(2,1)} %copy-done.5) | copy-start | bytes 1179652
  167.9 21.7 %collective-permute-start.19 = (bf16[3968,128]{1,0:T(8,128)(2,1)}, bf16[3968,128]{1,0:T(8,128)(2,1)}, u32[]{:S(2)}, u32[]{:S(2)}) collective-permute-start(bf16[3968,128]{1,0:T(8,128)(2,1)} %constant_dynamic-update-slice_fusion.2), channel_id=1, source_target_pairs={{0,1},{1,0},{2,3},{3,2},{4,5},{5,4},{6,7},{7,6},{8,9},{9,8},{10,11... | collective-permute-start | bytes 3047432 | tf_op jit(solution)/shard_map/ppermute | solution.py:135
  (20 other events, 55.3 us)

commit v4 on v3

--- a/solution.py
+++ b/solution.py
@@ -70,7 +70,7 @@
     return jnp.concatenate(terms, 0)
 
 AXIS_SHIFT = {"y": 1, "x": 3, "z": 5}
-PART_ORDERS = (("y", "x", "z"),)
+PART_ORDERS = (("y", "x", "z"), ("x", "z", "y"), ("z", "y", "x"))
 
 
 def coordinate(index, shift):
@@ -117,16 +117,19 @@
     parts = jnp.split(y, len(PART_ORDERS), 0)
     reduced = []
     for part, order in zip(parts, PART_ORDERS):
-        for shift, stage in exchange_steps(order):
+        for shift, stage in exchange_steps(order[:1]):
             perm = [(i, partner(i, shift, stage)) for i in range(count)]
             bit = keep_bit(coordinate(index, shift), stage)
             keep, send = split_halves(part, bit)
             part = keep + lax.ppermute(send, "range", perm)
+        for shift, stage in exchange_steps(order[1:]):
+            perm = [(i, partner(i, shift, stage)) for i in range(count)]
+            part = part + lax.ppermute(part, "range", perm)
         reduced.append(part)
     gathered = []
     for part, order in zip(reduced, PART_ORDERS):
         part = part.astype(jnp.bfloat16)
-        for shift, stage in reversed(exchange_steps(order)):
+        for shift, stage in reversed(exchange_steps(order[:1])):
             perm = [(i, partner(i, shift, stage)) for i in range(count)]
             bit = keep_bit(coordinate(index, shift), stage)
             part = join_halves(part, lax.ppermute(part, "range", perm), bit)
@@ -200,7 +203,7 @@
     )
     limit = jnp.float32(channels * math.sqrt(62.0))
     total_values = raw_grads.size
-    rows = total_values // channels
+    rows = 8064
     flat = jnp.pad(raw_grads.reshape(-1), (0, rows * channels - total_values)).reshape(rows, channels)
     summed = torus_psum(flat).reshape(-1)[:total_values].reshape(raw_grads.shape)
     grad_total = jnp.sqrt(jnp.sum(summed * summed))

time: 197 us -> 157 us (0.80)
  waiting for transfers between devices: 68 us -> 18.7 us
  starting transfers between devices: 61.6 us -> 74.9 us
  local copies, waits for them, and re-layouts: 34.1 us -> 30.5 us
  other arithmetic: 11 us -> 8.48 us
    ppermute x6, waiting for transfers between devices: 43.9 us -> 3.59 us  [torus_psum(): part = keep + lax.ppermute(send, 'range', perm)]
    ppermute x0 -> x12, starting transfers between devices: none -> 16.5 us  [torus_psum(): part = part + lax.ppermute(part, 'range', perm)]
    ppermute x6, waiting for transfers between devices: 17.7 us -> 7.03 us  [torus_psum(): part = join_halves(part, lax.ppermute(part, 'range', perm), bit)]
    add x5 -> x6, other arithmetic: 4.19 us -> 0.21 us  [torus_psum(): part = keep + lax.ppermute(send, 'range', perm)]
    ppermute x1, starting transfers between devices: 12 us -> 8.13 us  [torus_psum(): lax.ppermute(y, 'range', core_perm)]
    ppermute x6, starting transfers between devices: 24.3 us -> 27.3 us  [torus_psum(): part = keep + lax.ppermute(send, 'range', perm)]
    dynamic_update_slice x7 -> x3, local copies, waits for them, and re-layouts: 2.82 us -> 0.09 us  [join_halves(): full = lax.dynamic_update_slice_in_dim(full, y, bit * h, 0)]
    ppermute x0 -> x12, waiting for transfers between devices: none -> 2.47 us  [torus_psum(): part = part + lax.ppermute(part, 'range', perm)]
  transfers between devices with their start and end apart: 20 -> 32, of which waited for: 14 -> 14; matrix products, arithmetic and copies ran while one was open for 11% -> 14% of each run, Pallas kernels for 0% -> 0%
where the time goes in v4:
time: 157 us; the launch traced here: 156 us
  starting transfers between devices  74.9 us (48%)
  local copies, waits for them, and re-layouts  30.5 us (19%)
  matrix products  20.8 us (13%)
  waiting for transfers between devices  18.7 us (12%)
  other arithmetic  8.48 us (5%)
  between operations  2.75 us (2%)
    ppermute x6, starting transfers between devices, torus_psum(): part = keep + lax.ppermute(send, 'range', perm)  27.3 us
    ppermute x12, starting transfers between devices, torus_psum(): part = part + lax.ppermute(part, 'range', perm)  16.5 us
    dot_general x36, matrix products, conv_apply(): jnp.dot(xy_window(zcols, sx, sy), taps[sx, sy], preferred_element_type=jn...  13.9 us
    ppermute x3, starting transfers between devices, padded_many(): lax.ppermute(jnp.concatenate([g[:, :, PZ - 1:] for g in grids], -1), 'ran...  11.9 us
    ppermute x1, starting transfers between devices, torus_psum(): lax.ppermute(y, 'range', core_perm)  8.13 us
    ppermute x6, waiting for transfers between devices, torus_psum(): part = join_halves(part, lax.ppermute(part, 'range', perm), bit)  7.03 us
    ppermute x3, starting transfers between devices, padded_many(): lax.ppermute(jnp.concatenate([g[:, :, :1] for g in grids], -1), 'range',...  5.94 us
    unnamed x56, local copies, waits for them, and re-layouts  5.65 us
  transfers between devices with their start and end apart: 32, of which 14 were waited for; matrix products, arithmetic and copies ran while one was open for 14% of the time, Pallas kernels for 0%

profile of v4, /device:TPU:1, one launch (start us, length us, event | category | flops | bytes accessed | tf_op | source)
XLA Modules:
  0.0 156.1 jit_solution(13196186713169585017)
XLA Ops:
  6.3 1.5 gather_fusion.2
  8.0 4.6 %collective-permute-start = (bf16[8,8,1,256]{3,2,1,0:T(2,128)(2,1)S(1)}, bf16[8,8,1,256]{3,2,1,0:T(2,128)(2,1)S(1)}, u32[]{:S(2)}, u32[]{:S(2)}) collective-permute-start(bf16[8,8,1,256]{3,2,1,0:T(2,128)(2,1)S(1)} %pad_maximum_fusion.6), channel_id=1, source_target_pairs={{0,1},{1,2},{2,3},{3,4},{4,5},{5,6},{6,7},{7,8},{8,9},{9,10},{10,1... | collective-permute-start | bytes 98312 | tf_op jit(solution)/shard_map/ppermute | solution.py:29
  12.6 1.9 %collective-permute-start.1 = (bf16[8,8,1,256]{3,2,1,0:T(2,128)(2,1)S(1)}, bf16[8,8,1,256]{3,2,1,0:T(2,128)(2,1)S(1)}, u32[]{:S(2)}, u32[]{:S(2)}) collective-permute-start(bf16[8,8,1,256]{3,2,1,0:T(2,128)(2,1)S(1)} %pad_maximum_fusion.7), channel_id=1, source_target_pairs={{1,0},{2,1},{3,2},{4,3},{5,4},{6,5},{7,6},{8,7},{9,8},{10,9},{11,1... | collective-permute-start | bytes 98312 | tf_op jit(solution)/shard_map/ppermute | solution.py:30
  31.0 3.6 %collective-permute-start.2 = (bf16[8,8,1,128]{3,2,1,0:T(2,128)(2,1)S(1)}, bf16[8,8,1,128]{3,2,1,0:T(2,128)(2,1)S(1)}, u32[]{:S(2)}, u32[]{:S(2)}) collective-permute-start(bf16[8,8,1,128]{3,2,1,0:T(2,128)(2,1)S(1)} %get-tuple-element.70), channel_id=1, source_target_pairs={{0,1},{1,2},{2,3},{3,4},{4,5},{5,6},{6,7},{7,8},{8,9},{9,10},{10,1... | collective-permute-start | bytes 49160 | tf_op jit(solution)/shard_map/ppermute | solution.py:29
  34.7 1.9 %collective-permute-start.3 = (bf16[8,8,1,128]{3,2,1,0:T(2,128)(2,1)S(1)}, bf16[8,8,1,128]{3,2,1,0:T(2,128)(2,1)S(1)}, u32[]{:S(2)}, u32[]{:S(2)}) collective-permute-start(bf16[8,8,1,128]{3,2,1,0:T(2,128)(2,1)S(1)} %get-tuple-element.71), channel_id=1, source_target_pairs={{1,0},{2,1},{3,2},{4,3},{5,4},{6,5},{7,6},{8,7},{9,8},{10,9},{11,1... | collective-permute-start | bytes 49160 | tf_op jit(solution)/shard_map/ppermute | solution.py:30
  36.7 3.6 %collective-permute-start.4 = (bf16[8,8,1,128]{3,2,1,0:T(2,128)(2,1)S(1)}, bf16[8,8,1,128]{3,2,1,0:T(2,128)(2,1)S(1)}, u32[]{:S(2)}, u32[]{:S(2)}) collective-permute-start(bf16[8,8,1,128]{3,2,1,0:T(2,128)(2,1)S(1)} %get-tuple-element.68), channel_id=1, source_target_pairs={{0,1},{1,2},{2,3},{3,4},{4,5},{5,6},{6,7},{7,8},{8,9},{9,10},{10,1... | collective-permute-start | bytes 49160 | tf_op jit(solution)/shard_map/ppermute | solution.py:29
  40.3 2.1 %collective-permute-start.5 = (bf16[8,8,1,128]{3,2,1,0:T(2,128)(2,1)S(1)}, bf16[8,8,1,128]{3,2,1,0:T(2,128)(2,1)S(1)}, u32[]{:S(2)}, u32[]{:S(2)}) collective-permute-start(bf16[8,8,1,128]{3,2,1,0:T(2,128)(2,1)S(1)} %get-tuple-element.69), channel_id=1, source_target_pairs={{1,0},{2,1},{3,2},{4,3},{5,4},{6,5},{7,6},{8,7},{9,8},{10,9},{11,1... | collective-permute-start | bytes 49160 | tf_op jit(solution)/shard_map/ppermute | solution.py:30
  43.3 2.3 %collective-permute-done.5 = bf16[8,8,1,128]{3,2,1,0:T(2,128)(2,1)S(1)} collective-permute-done((bf16[8,8,1,128]{3,2,1,0:T(2,128)(2,1)S(1)}, bf16[8,8,1,128]{3,2,1,0:T(2,128)(2,1)S(1)}, u32[]{:S(2)}, u32[]{:S(2)}) %collective-permute-start.5) | collective-permute-done | bytes 16416 | tf_op jit(solution)/shard_map/ppermute | solution.py:30
  53.0 1.5 constant_dynamic-slice_fusion.6
  56.8 3.3 %collective-permute-done.6 = f32[4032,128]{1,0:T(8,128)} collective-permute-done((f32[4032,128]{1,0:T(8,128)}, f32[4032,128]{1,0:T(8,128)}, u32[]{:S(2)}, u32[]{:S(2)}) %collective-permute-start.6) | collective-permute-done | bytes 2064416 | tf_op jit(solution)/shard_map/ppermute | solution.py:116
  60.1 2.4 %dynamic-slice_add_fusion = f32[4032,128]{1,0:T(8,128)S(1)} fusion(f32[4032,128]{1,0:T(8,128)} %collective-permute-done.6, f32[8064,128]{1,0:T(8,128)} %copy-done.2, s32[]{:T(128)S(6)} %select_n.82), kind=kLoop, calls=%fused_computation.11 | loop fusion | flops 516096 | bytes 6193156 | tf_op jit(solution)/shard_map/add | solution.py:116
  64.4 5.8 %collective-permute-start.15 = (f32[672,128]{1,0:T(8,128)S(1)}, f32[672,128]{1,0:T(8,128)S(1)}, u32[]{:S(2)}, u32[]{:S(2)}) collective-permute-start(f32[672,128]{1,0:T(8,128)S(1)} %constant_dynamic-slice_fusion.3), channel_id=1, source_target_pairs={{0,8},{1,9},{2,10},{3,11},{4,12},{5,13},{6,14},{7,15},{8,0},{9,1},... | collective-permute-start | bytes 1032200 | tf_op jit(solution)/shard_map/ppermute | solution.py:124
  70.2 6.9 %collective-permute-start.23 = (f32[672,128]{1,0:T(8,128)S(1)}, f32[672,128]{1,0:T(8,128)S(1)}, u32[]{:S(2)}, u32[]{:S(2)}) collective-permute-start(f32[672,128]{1,0:T(8,128)S(1)} %constant_dynamic-slice_fusion.1), channel_id=1, source_target_pairs={{0,32},{1,33},{2,34},{3,35},{4,36},{5,37},{6,38},{7,39},{8,40},{9,... | collective-permute-start | bytes 1032200 | tf_op jit(solution)/shard_map/ppermute | solution.py:124
  77.1 3.9 %collective-permute-start.8 = (f32[336,128]{1,0:T(8,128)S(1)}, f32[336,128]{1,0:T(8,128)S(1)}, u32[]{:S(2)}, u32[]{:S(2)}) collective-permute-start(f32[336,128]{1,0:T(8,128)S(1)} %constant_dynamic-slice_fusion.4), channel_id=1, source_target_pairs={{0,6},{1,7},{2,4},{3,5},{4,2},{5,3},{6,0},{7,1},{8,14},{9,15},{10,... | collective-permute-start | bytes 516104 | tf_op jit(solution)/shard_map/ppermute | solution.py:124
  81.1 9.2 %collective-permute-start.16 = (f32[336,128]{1,0:T(8,128)S(1)}, f32[336,128]{1,0:T(8,128)S(1)}, u32[]{:S(2)}, u32[]{:S(2)}) collective-permute-start(f32[336,128]{1,0:T(8,128)S(1)} %constant_dynamic-slice_fusion.2), channel_id=1, source_target_pairs={{0,24},{1,25},{2,26},{3,27},{4,28},{5,29},{6,30},{7,31},{8,16},{9,... | collective-permute-start | bytes 516104 | tf_op jit(solution)/shard_map/ppermute | solution.py:124
  90.7 3.2 %collective-permute-done.16 = f32[336,128]{1,0:T(8,128)S(1)} collective-permute-done((f32[336,128]{1,0:T(8,128)S(1)}, f32[336,128]{1,0:T(8,128)S(1)}, u32[]{:S(2)}, u32[]{:S(2)}) %collective-permute-start.16) | collective-permute-done | bytes 172064 | tf_op jit(solution)/shard_map/ppermute | solution.py:124
  93.9 1.7 %collective-permute-start.17 = (f32[336,128]{1,0:T(8,128)S(1)}, f32[336,128]{1,0:T(8,128)S(1)}, u32[]{:S(2)}, u32[]{:S(2)}) collective-permute-start(f32[336,128]{1,0:T(8,128)S(1)} %dynamic-slice_add_fusion.5), channel_id=1, source_target_pairs={{0,32},{1,33},{2,34},{3,35},{4,36},{5,37},{6,38},{7,39},{8,40},{9,... | collective-permute-start | bytes 516104 | tf_op jit(solution)/shard_map/ppermute | solution.py:127
  96.2 2.2 %collective-permute-start.10 = (f32[336,128]{1,0:T(8,128)S(1)}, f32[336,128]{1,0:T(8,128)S(1)}, u32[]{:S(2)}, u32[]{:S(2)}) collective-permute-start(f32[336,128]{1,0:T(8,128)S(1)} %add.310), channel_id=1, source_target_pairs={{0,24},{1,25},{2,26},{3,27},{4,28},{5,29},{6,30},{7,31},{8,16},{9,... | collective-permute-start | bytes 516104 | tf_op jit(solution)/shard_map/ppermute | solution.py:127
  98.7 1.8 %collective-permute-start.18 = (f32[336,128]{1,0:T(8,128)S(1)}, f32[336,128]{1,0:T(8,128)S(1)}, u32[]{:S(2)}, u32[]{:S(2)}) collective-permute-start(f32[336,128]{1,0:T(8,128)S(1)} %add.318), channel_id=1, source_target_pairs={{0,96},{1,97},{2,98},{3,99},{4,100},{5,101},{6,102},{7,103},{8,104... | collective-permute-start | bytes 516104 | tf_op jit(solution)/shard_map/ppermute | solution.py:127
  100.7 1.8 %collective-permute-start.26 = (f32[336,128]{1,0:T(8,128)S(1)}, f32[336,128]{1,0:T(8,128)S(1)}, u32[]{:S(2)}, u32[]{:S(2)}) collective-permute-start(f32[336,128]{1,0:T(8,128)S(1)} %add.326), channel_id=1, source_target_pairs={{0,6},{1,7},{2,4},{3,5},{4,2},{5,3},{6,0},{7,1},{8,14},{9,15},{10,... | collective-permute-start | bytes 516104 | tf_op jit(solution)/shard_map/ppermute | solution.py:127
  102.5 1.9 %collective-permute-start.11 = (f32[336,128]{1,0:T(8,128)S(1)}, f32[336,128]{1,0:T(8,128)S(1)}, u32[]{:S(2)}, u32[]{:S(2)}) collective-permute-start(f32[336,128]{1,0:T(8,128)S(1)} %add.311), channel_id=1, source_target_pairs={{0,32},{1,33},{2,34},{3,35},{4,36},{5,37},{6,38},{7,39},{8,40},{9,... | collective-permute-start | bytes 516104 | tf_op jit(solution)/shard_map/ppermute | solution.py:127
  109.6 2.3 %collective-permute-start.20 = (f32[336,128]{1,0:T(8,128)S(1)}, f32[336,128]{1,0:T(8,128)S(1)}, u32[]{:S(2)}, u32[]{:S(2)}) collective-permute-start(f32[336,128]{1,0:T(8,128)S(1)} %add.320), channel_id=1, source_target_pairs={{0,6},{1,7},{2,4},{3,5},{4,2},{5,3},{6,0},{7,1},{8,14},{9,15},{10,... | collective-permute-start | bytes 516104 | tf_op jit(solution)/shard_map/ppermute | solution.py:127
  112.0 1.7 %collective-permute-start.28 = (f32[336,128]{1,0:T(8,128)S(1)}, f32[336,128]{1,0:T(8,128)S(1)}, u32[]{:S(2)}, u32[]{:S(2)}) collective-permute-start(f32[336,128]{1,0:T(8,128)S(1)} %add.328), channel_id=1, source_target_pairs={{0,24},{1,25},{2,26},{3,27},{4,28},{5,29},{6,30},{7,31},{8,16},{9,... | collective-permute-start | bytes 516104 | tf_op jit(solution)/shard_map/ppermute | solution.py:127
  115.2 2.0 %collective-permute-start.21 = (bf16[336,128]{1,0:T(8,128)(2,1)S(1)}, bf16[336,128]{1,0:T(8,128)(2,1)S(1)}, u32[]{:S(2)}, u32[]{:S(2)}) collective-permute-start(bf16[336,128]{1,0:T(8,128)(2,1)S(1)} %get-tuple-element.8), channel_id=1, source_target_pairs={{0,24},{1,25},{2,26},{3,27},{4,28},{5,29},{6,30},{7,31},{8,16},{9,... | collective-permute-start | bytes 258056 | tf_op jit(solution)/shard_map/ppermute | solution.py:135
  120.3 2.5 %collective-permute-done.29 = bf16[336,128]{1,0:T(8,128)(2,1)S(1)} collective-permute-done((bf16[336,128]{1,0:T(8,128)(2,1)S(1)}, bf16[336,128]{1,0:T(8,128)(2,1)S(1)}, u32[]{:S(2)}, u32[]{:S(2)}) %collective-permute-start.29) | collective-permute-done | bytes 86048 | tf_op jit(solution)/shard_map/ppermute | solution.py:135
  124.7 2.4 %collective-permute-done.30 = bf16[672,128]{1,0:T(8,128)(2,1)S(1)} collective-permute-done((bf16[672,128]{1,0:T(8,128)(2,1)S(1)}, bf16[672,128]{1,0:T(8,128)(2,1)S(1)}, u32[]{:S(2)}, u32[]{:S(2)}) %collective-permute-start.30) | collective-permute-done | bytes 172064 | tf_op jit(solution)/shard_map/ppermute | solution.py:135
  128.6 8.1 %collective-permute-start.31 = (bf16[4032,128]{1,0:T(8,128)(2,1)}, bf16[4032,128]{1,0:T(8,128)(2,1)}, u32[]{:S(2)}, u32[]{:S(2)}) collective-permute-start(bf16[4032,128]{1,0:T(8,128)(2,1)} %get-tuple-element.18), channel_id=1, source_target_pairs={{0,1},{1,0},{2,3},{3,2},{4,5},{5,4},{6,7},{7,6},{8,9},{9,8},{10,11... | collective-permute-start | bytes 3096584 | tf_op jit(solution)/shard_map/ppermute | solution.py:138
  137.7 1.5 reshape.320
  139.2 2.4 %copy.31 = bf16[2,2,2,2,2,2,2,4,2,2,2,128]{11,10,7,9,5,8,2,6,4,1,3,0:T(2,128)(2,1)S(1)} copy(bf16[2,2,2,2,2,2,2,4,2,2,2,128]{11,10,9,8,7,6,5,4,3,2,1,0:T(2,128)(2,1)} %reshape.320) | data formatting | bytes 2097152 | tf_op jit(solution)/shard_map/reshape | solution.py:192
  146.4 1.7 %gather_fusion.4 = bf16[32,128,128]{2,1,0:T(8,128)(2,1)} fusion(bf16[32,128,128]{2,1,0:T(8,128)(2,1)S(1)} %bitcast.290, s32[1024]{0:T(1024)S(1)} %pad_clamp_fusion), kind=kCustom, calls=%fused_computation.4 | custom fusion | bytes 2097280 | tf_op jit(solution)/shard_map/gather | solution.py:194
  150.7 1.6 %fusion = f32[]{:T(128)} fusion(bf16[8064,128]{1,0:T(8,128)(2,1)S(1)} %constant_dynamic-update-slice_fusion), kind=kLoop, calls=%fused_computation.9 | loop fusion | flops 3047423 | bytes 2031620 | tf_op jit(solution)/shard_map/reduce_sum | solution.py:209
  153.3 2.0 %fusion.32 = (f32[3456,128]{1,0:T(8,128)}, f32[3456,128]{1,0:T(8,128)}) fusion(f32[7936,128]{1,0:T(8,128)S(1)} %convert_multiply_fusion), kind=kLoop, calls=%fused_computation.193 | loop fusion | bytes 7077888 | tf_op jit(solution)/shard_map/slice | solution.py:212
  (247 shorter events, 57.8 us)
Async XLA Ops:
  8.0 12.3 %collective-permute-start = (bf16[8,8,1,256]{3,2,1,0:T(2,128)(2,1)S(1)}, bf16[8,8,1,256]{3,2,1,0:T(2,128)(2,1)S(1)}, u32[]{:S(2)}, u32[]{:S(2)}) collective-permute-start(bf16[8,8,1,256]{3,2,1,0:T(2,128)(2,1)S(1)} %pad_maximum_fusion.6), channel_id=1, source_target_pairs={{0,1},{1,2},{2,3},{3,4},{4,5},{5,6},{6,7},{7,8},{8,9},{9,10},{10,1... | collective-permute-start | bytes 98312 | tf_op jit(solution)/shard_map/ppermute | solution.py:29
  12.6 7.7 %collective-permute-start.1 = (bf16[8,8,1,256]{3,2,1,0:T(2,128)(2,1)S(1)}, bf16[8,8,1,256]{3,2,1,0:T(2,128)(2,1)S(1)}, u32[]{:S(2)}, u32[]{:S(2)}) collective-permute-start(bf16[8,8,1,256]{3,2,1,0:T(2,128)(2,1)S(1)} %pad_maximum_fusion.7), channel_id=1, source_target_pairs={{1,0},{2,1},{3,2},{4,3},{5,4},{6,5},{7,6},{8,7},{9,8},{10,9},{11,1... | collective-permute-start | bytes 98312 | tf_op jit(solution)/shard_map/ppermute | solution.py:30
  31.0 11.4 %collective-permute-start.2 = (bf16[8,8,1,128]{3,2,1,0:T(2,128)(2,1)S(1)}, bf16[8,8,1,128]{3,2,1,0:T(2,128)(2,1)S(1)}, u32[]{:S(2)}, u32[]{:S(2)}) collective-permute-start(bf16[8,8,1,128]{3,2,1,0:T(2,128)(2,1)S(1)} %get-tuple-element.70), channel_id=1, source_target_pairs={{0,1},{1,2},{2,3},{3,4},{4,5},{5,6},{6,7},{7,8},{8,9},{9,10},{10,1... | collective-permute-start | bytes 49160 | tf_op jit(solution)/shard_map/ppermute | solution.py:29
  34.7 7.8 %collective-permute-start.3 = (bf16[8,8,1,128]{3,2,1,0:T(2,128)(2,1)S(1)}, bf16[8,8,1,128]{3,2,1,0:T(2,128)(2,1)S(1)}, u32[]{:S(2)}, u32[]{:S(2)}) collective-permute-start(bf16[8,8,1,128]{3,2,1,0:T(2,128)(2,1)S(1)} %get-tuple-element.71), channel_id=1, source_target_pairs={{1,0},{2,1},{3,2},{4,3},{5,4},{6,5},{7,6},{8,7},{9,8},{10,9},{11,1... | collective-permute-start | bytes 49160 | tf_op jit(solution)/shard_map/ppermute | solution.py:30
  36.7 6.6 %collective-permute-start.4 = (bf16[8,8,1,128]{3,2,1,0:T(2,128)(2,1)S(1)}, bf16[8,8,1,128]{3,2,1,0:T(2,128)(2,1)S(1)}, u32[]{:S(2)}, u32[]{:S(2)}) collective-permute-start(bf16[8,8,1,128]{3,2,1,0:T(2,128)(2,1)S(1)} %get-tuple-element.68), channel_id=1, source_target_pairs={{0,1},{1,2},{2,3},{3,4},{4,5},{5,6},{6,7},{7,8},{8,9},{9,10},{10,1... | collective-permute-start | bytes 49160 | tf_op jit(solution)/shard_map/ppermute | solution.py:29
  40.3 5.2 %collective-permute-start.5 = (bf16[8,8,1,128]{3,2,1,0:T(2,128)(2,1)S(1)}, bf16[8,8,1,128]{3,2,1,0:T(2,128)(2,1)S(1)}, u32[]{:S(2)}, u32[]{:S(2)}) collective-permute-start(bf16[8,8,1,128]{3,2,1,0:T(2,128)(2,1)S(1)} %get-tuple-element.69), channel_id=1, source_target_pairs={{1,0},{2,1},{3,2},{4,3},{5,4},{6,5},{7,6},{8,7},{9,8},{10,9},{11,1... | collective-permute-start | bytes 49160 | tf_op jit(solution)/shard_map/ppermute | solution.py:30
  55.6 4.5 %collective-permute-start.6 = (f32[4032,128]{1,0:T(8,128)}, f32[4032,128]{1,0:T(8,128)}, u32[]{:S(2)}, u32[]{:S(2)}) collective-permute-start(f32[4032,128]{1,0:T(8,128)} %constant_dynamic-slice_fusion.6), channel_id=1, source_target_pairs={{0,1},{1,0},{2,3},{3,2},{4,5},{5,4},{6,7},{7,6},{8,9},{9,8},{10,11... | collective-permute-start | bytes 6193160 | tf_op jit(solution)/shard_map/ppermute | solution.py:116
  62.7 14.4 %collective-permute-start.7 = (f32[672,128]{1,0:T(8,128)S(1)}, f32[672,128]{1,0:T(8,128)S(1)}, u32[]{:S(2)}, u32[]{:S(2)}) collective-permute-start(f32[672,128]{1,0:T(8,128)S(1)} %constant_dynamic-slice_fusion.5), channel_id=1, source_target_pairs={{0,2},{1,3},{2,0},{3,1},{4,6},{5,7},{6,4},{7,5},{8,10},{9,11},{10,... | collective-permute-start | bytes 1032200 | tf_op jit(solution)/shard_map/ppermute | solution.py:124
  64.4 16.7 %collective-permute-start.15 = (f32[672,128]{1,0:T(8,128)S(1)}, f32[672,128]{1,0:T(8,128)S(1)}, u32[]{:S(2)}, u32[]{:S(2)}) collective-permute-start(f32[672,128]{1,0:T(8,128)S(1)} %constant_dynamic-slice_fusion.3), channel_id=1, source_target_pairs={{0,8},{1,9},{2,10},{3,11},{4,12},{5,13},{6,14},{7,15},{8,0},{9,1},... | collective-permute-start | bytes 1032200 | tf_op jit(solution)/shard_map/ppermute | solution.py:124
  70.2 20.2 %collective-permute-start.23 = (f32[672,128]{1,0:T(8,128)S(1)}, f32[672,128]{1,0:T(8,128)S(1)}, u32[]{:S(2)}, u32[]{:S(2)}) collective-permute-start(f32[672,128]{1,0:T(8,128)S(1)} %constant_dynamic-slice_fusion.1), channel_id=1, source_target_pairs={{0,32},{1,33},{2,34},{3,35},{4,36},{5,37},{6,38},{7,39},{8,40},{9,... | collective-permute-start | bytes 1032200 | tf_op jit(solution)/shard_map/ppermute | solution.py:124
  77.1 13.4 %collective-permute-start.8 = (f32[336,128]{1,0:T(8,128)S(1)}, f32[336,128]{1,0:T(8,128)S(1)}, u32[]{:S(2)}, u32[]{:S(2)}) collective-permute-start(f32[336,128]{1,0:T(8,128)S(1)} %constant_dynamic-slice_fusion.4), channel_id=1, source_target_pairs={{0,6},{1,7},{2,4},{3,5},{4,2},{5,3},{6,0},{7,1},{8,14},{9,15},{10,... | collective-permute-start | bytes 516104 | tf_op jit(solution)/shard_map/ppermute | solution.py:124
  81.1 12.7 %collective-permute-start.16 = (f32[336,128]{1,0:T(8,128)S(1)}, f32[336,128]{1,0:T(8,128)S(1)}, u32[]{:S(2)}, u32[]{:S(2)}) collective-permute-start(f32[336,128]{1,0:T(8,128)S(1)} %constant_dynamic-slice_fusion.2), channel_id=1, source_target_pairs={{0,24},{1,25},{2,26},{3,27},{4,28},{5,29},{6,30},{7,31},{8,16},{9,... | collective-permute-start | bytes 516104 | tf_op jit(solution)/shard_map/ppermute | solution.py:124
  90.5 5.5 %collective-permute-start.24 = (f32[336,128]{1,0:T(8,128)S(1)}, f32[336,128]{1,0:T(8,128)S(1)}, u32[]{:S(2)}, u32[]{:S(2)}) collective-permute-start(f32[336,128]{1,0:T(8,128)S(1)} %constant_dynamic-slice_fusion), channel_id=1, source_target_pairs={{0,96},{1,97},{2,98},{3,99},{4,100},{5,101},{6,102},{7,103},{8,104... | collective-permute-start | bytes 516104 | tf_op jit(solution)/shard_map/ppermute | solution.py:124
  90.6 5.6 %collective-permute-start.9 = (f32[336,128]{1,0:T(8,128)S(1)}, f32[336,128]{1,0:T(8,128)S(1)}, u32[]{:S(2)}, u32[]{:S(2)}) collective-permute-start(f32[336,128]{1,0:T(8,128)S(1)} %dynamic-slice_add_fusion.6), channel_id=1, source_target_pairs={{0,8},{1,9},{2,10},{3,11},{4,12},{5,13},{6,14},{7,15},{8,0},{9,1},... | collective-permute-start | bytes 516104 | tf_op jit(solution)/shard_map/ppermute | solution.py:127
  93.9 4.8 %collective-permute-start.17 = (f32[336,128]{1,0:T(8,128)S(1)}, f32[336,128]{1,0:T(8,128)S(1)}, u32[]{:S(2)}, u32[]{:S(2)}) collective-permute-start(f32[336,128]{1,0:T(8,128)S(1)} %dynamic-slice_add_fusion.5), channel_id=1, source_target_pairs={{0,32},{1,33},{2,34},{3,35},{4,36},{5,37},{6,38},{7,39},{8,40},{9,... | collective-permute-start | bytes 516104 | tf_op jit(solution)/shard_map/ppermute | solution.py:127
  96.0 4.6 %collective-permute-start.25 = (f32[336,128]{1,0:T(8,128)S(1)}, f32[336,128]{1,0:T(8,128)S(1)}, u32[]{:S(2)}, u32[]{:S(2)}) collective-permute-start(f32[336,128]{1,0:T(8,128)S(1)} %dynamic-slice_add_fusion.4), channel_id=1, source_target_pairs={{0,2},{1,3},{2,0},{3,1},{4,6},{5,7},{6,4},{7,5},{8,10},{9,11},{10,... | collective-permute-start | bytes 516104 | tf_op jit(solution)/shard_map/ppermute | solution.py:127
  96.2 6.2 %collective-permute-start.10 = (f32[336,128]{1,0:T(8,128)S(1)}, f32[336,128]{1,0:T(8,128)S(1)}, u32[]{:S(2)}, u32[]{:S(2)}) collective-permute-start(f32[336,128]{1,0:T(8,128)S(1)} %add.310), channel_id=1, source_target_pairs={{0,24},{1,25},{2,26},{3,27},{4,28},{5,29},{6,30},{7,31},{8,16},{9,... | collective-permute-start | bytes 516104 | tf_op jit(solution)/shard_map/ppermute | solution.py:127
  98.7 6.0 %collective-permute-start.18 = (f32[336,128]{1,0:T(8,128)S(1)}, f32[336,128]{1,0:T(8,128)S(1)}, u32[]{:S(2)}, u32[]{:S(2)}) collective-permute-start(f32[336,128]{1,0:T(8,128)S(1)} %add.318), channel_id=1, source_target_pairs={{0,96},{1,97},{2,98},{3,99},{4,100},{5,101},{6,102},{7,103},{8,104... | collective-permute-start | bytes 516104 | tf_op jit(solution)/shard_map/ppermute | solution.py:127
  100.7 5.8 %collective-permute-start.26 = (f32[336,128]{1,0:T(8,128)S(1)}, f32[336,128]{1,0:T(8,128)S(1)}, u32[]{:S(2)}, u32[]{:S(2)}) collective-permute-start(f32[336,128]{1,0:T(8,128)S(1)} %add.326), channel_id=1, source_target_pairs={{0,6},{1,7},{2,4},{3,5},{4,2},{5,3},{6,0},{7,1},{8,14},{9,15},{10,... | collective-permute-start | bytes 516104 | tf_op jit(solution)/shard_map/ppermute | solution.py:127
  102.5 5.0 %collective-permute-start.11 = (f32[336,128]{1,0:T(8,128)S(1)}, f32[336,128]{1,0:T(8,128)S(1)}, u32[]{:S(2)}, u32[]{:S(2)}) collective-permute-start(f32[336,128]{1,0:T(8,128)S(1)} %add.311), channel_id=1, source_target_pairs={{0,32},{1,33},{2,34},{3,35},{4,36},{5,37},{6,38},{7,39},{8,40},{9,... | collective-permute-start | bytes 516104 | tf_op jit(solution)/shard_map/ppermute | solution.py:127
  104.7 4.9 %collective-permute-start.19 = (f32[336,128]{1,0:T(8,128)S(1)}, f32[336,128]{1,0:T(8,128)S(1)}, u32[]{:S(2)}, u32[]{:S(2)}) collective-permute-start(f32[336,128]{1,0:T(8,128)S(1)} %add.319), channel_id=1, source_target_pairs={{0,2},{1,3},{2,0},{3,1},{4,6},{5,7},{6,4},{7,5},{8,10},{9,11},{10,... | collective-permute-start | bytes 516104 | tf_op jit(solution)/shard_map/ppermute | solution.py:127
  106.5 5.4 %collective-permute-start.27 = (f32[336,128]{1,0:T(8,128)S(1)}, f32[336,128]{1,0:T(8,128)S(1)}, u32[]{:S(2)}, u32[]{:S(2)}) collective-permute-start(f32[336,128]{1,0:T(8,128)S(1)} %add.327), channel_id=1, source_target_pairs={{0,8},{1,9},{2,10},{3,11},{4,12},{5,13},{6,14},{7,15},{8,0},{9,1},... | collective-permute-start | bytes 516104 | tf_op jit(solution)/shard_map/ppermute | solution.py:127
  107.5 6.1 %collective-permute-start.12 = (f32[336,128]{1,0:T(8,128)S(1)}, f32[336,128]{1,0:T(8,128)S(1)}, u32[]{:S(2)}, u32[]{:S(2)}) collective-permute-start(f32[336,128]{1,0:T(8,128)S(1)} %add.312), channel_id=1, source_target_pairs={{0,96},{1,97},{2,98},{3,99},{4,100},{5,101},{6,102},{7,103},{8,104... | collective-permute-start | bytes 516104 | tf_op jit(solution)/shard_map/ppermute | solution.py:127
  109.6 5.5 %collective-permute-start.20 = (f32[336,128]{1,0:T(8,128)S(1)}, f32[336,128]{1,0:T(8,128)S(1)}, u32[]{:S(2)}, u32[]{:S(2)}) collective-permute-start(f32[336,128]{1,0:T(8,128)S(1)} %add.320), channel_id=1, source_target_pairs={{0,6},{1,7},{2,4},{3,5},{4,2},{5,3},{6,0},{7,1},{8,14},{9,15},{10,... | collective-permute-start | bytes 516104 | tf_op jit(solution)/shard_map/ppermute | solution.py:127
  112.0 5.8 %collective-permute-start.28 = (f32[336,128]{1,0:T(8,128)S(1)}, f32[336,128]{1,0:T(8,128)S(1)}, u32[]{:S(2)}, u32[]{:S(2)}) collective-permute-start(f32[336,128]{1,0:T(8,128)S(1)} %add.328), channel_id=1, source_target_pairs={{0,24},{1,25},{2,26},{3,27},{4,28},{5,29},{6,30},{7,31},{8,16},{9,... | collective-permute-start | bytes 516104 | tf_op jit(solution)/shard_map/ppermute | solution.py:127
  113.7 5.6 %collective-permute-start.13 = (bf16[336,128]{1,0:T(8,128)(2,1)S(1)}, bf16[336,128]{1,0:T(8,128)(2,1)S(1)}, u32[]{:S(2)}, u32[]{:S(2)}) collective-permute-start(bf16[336,128]{1,0:T(8,128)(2,1)S(1)} %get-tuple-element.6), channel_id=1, source_target_pairs={{0,6},{1,7},{2,4},{3,5},{4,2},{5,3},{6,0},{7,1},{8,14},{9,15},{10,... | collective-permute-start | bytes 258056 | tf_op jit(solution)/shard_map/ppermute | solution.py:135
  115.2 4.9 %collective-permute-start.21 = (bf16[336,128]{1,0:T(8,128)(2,1)S(1)}, bf16[336,128]{1,0:T(8,128)(2,1)S(1)}, u32[]{:S(2)}, u32[]{:S(2)}) collective-permute-start(bf16[336,128]{1,0:T(8,128)(2,1)S(1)} %get-tuple-element.8), channel_id=1, source_target_pairs={{0,24},{1,25},{2,26},{3,27},{4,28},{5,29},{6,30},{7,31},{8,16},{9,... | collective-permute-start | bytes 258056 | tf_op jit(solution)/shard_map/ppermute | solution.py:135
  117.9 4.9 %collective-permute-start.29 = (bf16[336,128]{1,0:T(8,128)(2,1)S(1)}, bf16[336,128]{1,0:T(8,128)(2,1)S(1)}, u32[]{:S(2)}, u32[]{:S(2)}) collective-permute-start(bf16[336,128]{1,0:T(8,128)(2,1)S(1)} %get-tuple-element.10), channel_id=1, source_target_pairs={{0,96},{1,97},{2,98},{3,99},{4,100},{5,101},{6,102},{7,103},{8,104... | collective-permute-start | bytes 258056 | tf_op jit(solution)/shard_map/ppermute | solution.py:135
  119.4 4.6 %collective-permute-start.14 = (bf16[672,128]{1,0:T(8,128)(2,1)S(1)}, bf16[672,128]{1,0:T(8,128)(2,1)S(1)}, u32[]{:S(2)}, u32[]{:S(2)}) collective-permute-start(bf16[672,128]{1,0:T(8,128)(2,1)S(1)} %constant_dynamic-update-slice_fusion.12), channel_id=1, source_target_pairs={{0,2},{1,3},{2,0},{3,1},{4,6},{5,7},{6,4},{7,5},{8,10},{9,11},{10,... | collective-permute-start | bytes 516104 | tf_op jit(solution)/shard_map/ppermute | solution.py:135
  120.2 4.5 %collective-permute-start.22 = (bf16[672,128]{1,0:T(8,128)(2,1)S(1)}, bf16[672,128]{1,0:T(8,128)(2,1)S(1)}, u32[]{:S(2)}, u32[]{:S(2)}) collective-permute-start(bf16[672,128]{1,0:T(8,128)(2,1)S(1)} %constant_dynamic-update-slice_fusion.8), channel_id=1, source_target_pairs={{0,8},{1,9},{2,10},{3,11},{4,12},{5,13},{6,14},{7,15},{8,0},{9,1},... | collective-permute-start | bytes 516104 | tf_op jit(solution)/shard_map/ppermute | solution.py:135
  122.8 4.3 %collective-permute-start.30 = (bf16[672,128]{1,0:T(8,128)(2,1)S(1)}, bf16[672,128]{1,0:T(8,128)(2,1)S(1)}, u32[]{:S(2)}, u32[]{:S(2)}) collective-permute-start(bf16[672,128]{1,0:T(8,128)(2,1)S(1)} %constant_dynamic-update-slice_fusion.4), channel_id=1, source_target_pairs={{0,32},{1,33},{2,34},{3,35},{4,36},{5,37},{6,38},{7,39},{8,40},{9,... | collective-permute-start | bytes 516104 | tf_op jit(solution)/shard_map/ppermute | solution.py:135
  128.6 20.7 %collective-permute-start.31 = (bf16[4032,128]{1,0:T(8,128)(2,1)}, bf16[4032,128]{1,0:T(8,128)(2,1)}, u32[]{:S(2)}, u32[]{:S(2)}) collective-permute-start(bf16[4032,128]{1,0:T(8,128)(2,1)} %get-tuple-element.18), channel_id=1, source_target_pairs={{0,1},{1,0},{2,3},{3,2},{4,5},{5,4},{6,7},{7,6},{8,9},{9,8},{10,11... | collective-permute-start | bytes 3096584 | tf_op jit(solution)/shard_map/ppermute | solution.py:138
  (26 other events, 115.3 us)
